TPU v7x, 32 devices: a whole 2x2x4 slice. The times are simulated.
32 devices in a mesh: band: 2 (over core), page: 16 (over z, y, x).
Axes of the slice: x: 2, y: 2, z: 4, core: 2. Of those that a mesh axis runs over, the one named last changes fastest.
Arguments:
- hidden: bfloat16 [48, 576, 768], P('page', 'band'), may hold values from -6 to 6
- cotangent: bfloat16 [48, 576, 768], P('page', 'band'), may hold values from -6 to 6
- page_lengths: int32 [48], P('page'), may hold values from 263 to 527, as said below
- x_coord: int32 [48, 576], P('page'), may hold values from 0 to 999
- line_ids: int32 [48, 576], P('page'), may hold values from 0 to 63, never falling along the last dimension, each value on 1 to 24 neighbouring positions
- qkv_w: bfloat16 [768, 2304], replicated, may hold values from -0.21875 to 0.21875
- q_bias: bfloat16 [768], replicated, may hold values from -3 to 3
- v_bias: bfloat16 [768], replicated, may hold values from -3 to 3
- rel_table: bfloat16 [32, 12], replicated, may hold values from -4 to 4
- x_table: bfloat16 [64, 12], replicated, may hold values from -4 to 4
- y_table: bfloat16 [64, 12], replicated, may hold values from -4 to 4
- out_w: bfloat16 [768, 768], replicated, may hold values from -0.875 to 0.875
- out_b: bfloat16 [768], replicated, may hold values from -1.75 to 1.75
- ln1_gain: bfloat16 [768], replicated, may hold values from 0.5 to 1.5
- ln1_bias: bfloat16 [768], replicated, may hold values from -1.75 to 1.75
- ffn_in_w: bfloat16 [768, 3072], replicated, may hold values from -0.21875 to 0.21875
- ffn_in_b: bfloat16 [3072], replicated, may hold values from -1.75 to 1.75
- ffn_out_w: bfloat16 [3072, 768], replicated, may hold values from -0.109375 to 0.109375
- ffn_out_b: bfloat16 [768], replicated, may hold values from -1.75 to 1.75
- ln2_gain: bfloat16 [768], replicated, may hold values from 0.5 to 1.5
- ln2_bias: bfloat16 [768], replicated, may hold values from -1.75 to 1.75
Outputs:
- output: bfloat16 [48, 576, 768], P('page', 'band')
- grad_hidden: float32 [48, 576, 768], P('page', 'band')
- grad_qkv_w: float32 [768, 2304], replicated
- grad_q_bias: float32 [768], replicated
- grad_v_bias: float32 [768], replicated
- grad_rel_table: float32 [32, 12], replicated
- grad_x_table: float32 [64, 12], replicated
- grad_y_table: float32 [64, 12], replicated
- grad_out_w: float32 [768, 768], replicated
- grad_out_b: float32 [768], replicated
- grad_ln1_gain: float32 [768], replicated
- grad_ln1_bias: float32 [768], replicated
- grad_ffn_in_w: float32 [768, 3072], P(None, ('band', 'page'))
- grad_ffn_in_b: float32 [3072], replicated
- grad_ffn_out_w: float32 [3072, 768], P(('band', 'page'))
- grad_ffn_out_b: float32 [768], replicated
- grad_ln2_gain: float32 [768], replicated
- grad_ln2_bias: float32 [768], replicated
Inputs may be any that keep to these rules, and one draw needn't show every extreme that they name: `page_lengths`: positions from 49 plus a page's length on are padding. Of the 3 pages held by each position of the `page` axis, one holds 527 text tokens. `line_ids`: along a page the line numbers never fall; a line holds 1 to 24 positions.
All inputs are finite; a program needn't handle non-finite values.
Results may differ from a plain program's by a relative error of at most 0.014.
Values may be sent and summed in bfloat16 or wider, within the bound.
No kernel may reach another device: no remote copies, remote signals or barrier semaphores. Data moves between devices by JAX's collectives and lax.ppermute only.
A program may use at most 256 MiB of HBM per device.

v0:
```python
import math

import jax
import jax.numpy as jnp
import numpy as np
from jax import lax
from jax.sharding import PartitionSpec as P

REL_BUCKETS = 32
REL_REACH = 128
XY_BUCKETS = 64
XY_REACH = 256
VIS_SIDE = 7
VIS = 49
HALF = 64


epsilon = 1e-05
line_gap = 15
masked_value = -1e30


def extended_2(cells, sides, width):
    for axis, dim in sides:
        count = lax.axis_size(axis)
        ends = count - 1
        head = lax.slice_in_dim(cells, 0, width, axis=dim)
        tail = lax.slice_in_dim(cells, cells.shape[dim] - width, cells.shape[dim], axis=dim)
        cells = jnp.concatenate(
            [
                lax.ppermute(tail, axis, [(i, (i + 1) % count) for i in range(ends)]),
                cells,
                lax.ppermute(head, axis, [((i + 1) % count, i) for i in range(ends)]),
            ],
            axis=dim,
        )
    return cells


def from_root(block, axis, owner):
    block = jnp.where(lax.axis_index(axis) == owner, block, jnp.zeros_like(block))
    return lax.psum(block, axis)


def shifted(block, axis, distance):
    devices = range(lax.axis_size(axis))
    route = [(i - distance, i) for i in devices if i - distance in devices]
    return lax.ppermute(block, axis, route)


def bucket_edges(buckets, reach_max):
    half_count = buckets // 2
    exact_count = half_count // 2
    spread = half_count - exact_count
    thresholds = []
    for step_level in range(1, spread):
        bound_value = exact_count * (reach_max / exact_count) ** (step_level / spread)
        thresholds.append(int(np.ceil(bound_value - 1e-09)))
    return thresholds


def bucketize(offsets, buckets, reach_max):
    half_count = buckets // 2
    distance = jnp.abs(offsets)
    result = jnp.minimum(distance, half_count // 2)
    for threshold in bucket_edges(buckets, reach_max):
        result = result + (distance >= threshold).astype(jnp.int32)
    return result + half_count * (offsets > 0).astype(jnp.int32)


def page_coords(x_coord, line_ids):
    position = jnp.arange(x_coord.shape[-1], dtype=jnp.int32)
    cell_size = 1000 // VIS_SIDE
    grid_x = position % VIS_SIDE * cell_size + cell_size // 2
    grid_y = position // VIS_SIDE * cell_size + cell_size // 2
    visual = position < VIS
    return (jnp.where(visual, grid_x, x_coord), jnp.where(visual, grid_y, line_ids * line_gap))


def allowed(query_pos, key_pos, lengths):
    keys_row = key_pos[None, :]
    queries_col = query_pos[:, None]
    in_reach = (keys_row < VIS) | (queries_col >= VIS) & (jnp.abs(queries_col - keys_row) <= HALF)
    key_live = (key_pos[None, None, :] >= 0) & (
        key_pos[None, None, :] < VIS + lengths[:, None, None]
    )
    return key_live & in_reach[None]


def band_geometry(band_index, band_rows, x_coord, line_ids, page_lengths):
    band_start = band_index * band_rows
    query_pos = band_start + jnp.arange(band_rows, dtype=jnp.int32)
    ext_pos = band_start - HALF + jnp.arange(band_rows + 2 * HALF, dtype=jnp.int32)
    visual_pos = jnp.arange(VIS, dtype=jnp.int32)
    visual_pos = jnp.where(visual_pos < band_start - HALF, visual_pos, -1)
    key_pos = jnp.concatenate([visual_pos, ext_pos])
    key_mask = allowed(query_pos, key_pos, page_lengths)
    coord_x, coord_y = page_coords(x_coord, line_ids)
    safe_pos = jnp.clip(key_pos, 0, x_coord.shape[1] - 1)
    ids_shape = (x_coord.shape[0], band_rows, key_pos.shape[0])
    rel_ids = bucketize(key_pos[None, :] - query_pos[:, None], REL_BUCKETS, REL_REACH)
    rel_ids = jnp.broadcast_to(rel_ids[None], ids_shape)

    def pair_ids(coords):
        query_coords = lax.dynamic_slice_in_dim(coords, band_start, band_rows, 1)
        key_coords = jnp.take(coords, safe_pos, axis=1)
        return bucketize(key_coords[:, None, :] - query_coords[:, :, None], XY_BUCKETS, XY_REACH)

    return (key_mask, (rel_ids, pair_ids(coord_x), pair_ids(coord_y)))


def one_hots(bucket_ids, table_rows):
    return (bucket_ids[..., None] == jnp.arange(table_rows, dtype=jnp.int32)).astype(jnp.bfloat16)


def score_bias(families, tables):
    running = None
    for bucket_ids, table in zip(families, tables):
        bias_term = jnp.einsum(
            "pqkc,ch->phqk",
            one_hots(bucket_ids, table.shape[0]),
            table,
            preferred_element_type=jnp.float32,
        )
        running = bias_term if running is None else running + bias_term
    return running


def table_grads(families, tables, grad_scores_low):
    grad_tables = []
    for bucket_ids, table in zip(families, tables):
        grad_tables.append(
            jnp.einsum(
                "phqk,pqkc->ch",
                grad_scores_low,
                one_hots(bucket_ids, table.shape[0]),
                preferred_element_type=jnp.float32,
            )
        )
    return grad_tables


def attention_scores(queries, key_heads, families, tables, key_mask, score_scale):
    raw_scores = (
        jnp.einsum("pqhd,pkhd->phqk", queries, key_heads, preferred_element_type=jnp.float32)
        * score_scale
    )
    raw_scores = raw_scores + score_bias(families, tables)
    return jnp.where(key_mask[:, None], raw_scores, masked_value)


def layer_norm_parts(running, norm_gain, norm_shift):
    row_mean = jnp.mean(running, axis=-1, keepdims=True)
    centred = running - row_mean
    inv_std = lax.rsqrt(jnp.mean(centred * centred, axis=-1, keepdims=True) + epsilon)
    normed = centred * inv_std
    return (normed * norm_gain + norm_shift, normed, inv_std)


def norm_back(grad_norm, normed, inv_std, norm_gain):
    scaled = grad_norm * norm_gain
    return inv_std * (
        scaled
        - jnp.mean(scaled, axis=-1, keepdims=True)
        - normed * jnp.mean(scaled * normed, axis=-1, keepdims=True)
    )


def gelu_slope(inner_pre):
    return 0.5 * (1.0 + lax.erf(inner_pre * 2.0 ** (-0.5))) + inner_pre * jnp.exp(
        -0.5 * inner_pre * inner_pre
    ) * (2.0 * math.pi) ** (-0.5)


def rows_product(left, right):
    return lax.dot_general(
        left, right, (((0,), (0,)), ((), ())), preferred_element_type=jnp.float32
    )


def local(
    hidden,
    cotangent,
    page_lengths,
    x_coord,
    line_ids,
    qkv_w,
    q_bias,
    v_bias,
    rel_table,
    x_table,
    y_table,
    out_w,
    out_b,
    ln1_gain,
    ln1_bias,
    ffn_in_w,
    ffn_in_b,
    ffn_out_w,
    ffn_out_b,
    ln2_gain,
    ln2_bias,
):
    page_count, band_rows, model_width = hidden.shape
    head_count = rel_table.shape[1]
    head_size = model_width // head_count
    score_scale = head_size ** (-0.5)
    row_count = page_count * band_rows
    tables = (rel_table, x_table, y_table)
    key_mask, families = band_geometry(
        lax.axis_index("band"), band_rows, x_coord, line_ids, page_lengths
    )
    tok_rows = hidden.reshape(row_count, model_width)
    mixed_bias = jnp.concatenate(
        [
            q_bias.astype(jnp.float32),
            jnp.zeros(q_bias.shape, jnp.float32),
            v_bias.astype(jnp.float32),
        ]
    )
    mixed_rows = (jnp.dot(tok_rows, qkv_w, preferred_element_type=jnp.float32) + mixed_bias).astype(
        jnp.bfloat16
    )
    queries = mixed_rows[:, :model_width].reshape(page_count, band_rows, head_count, head_size)
    pair_rows = mixed_rows[:, model_width:].reshape(page_count, band_rows, 2 * model_width)
    extended = extended_2(pair_rows, (("band", 1),), HALF)
    visual_pairs = from_root(pair_rows[:, :VIS], "band", 0)
    key_rows = jnp.concatenate([visual_pairs, extended], axis=1)
    key_count = key_rows.shape[1]
    key_heads = key_rows[..., :model_width].reshape(page_count, key_count, head_count, head_size)
    value_heads = key_rows[..., model_width:].reshape(page_count, key_count, head_count, head_size)
    scores = attention_scores(queries, key_heads, families, tables, key_mask, score_scale)
    row_peak = jnp.max(scores, axis=-1, keepdims=True)
    log_total = row_peak + jnp.log(jnp.sum(jnp.exp(scores - row_peak), axis=-1, keepdims=True))
    weights = jnp.exp(scores - log_total)
    weights_low = weights.astype(jnp.bfloat16)
    context = jnp.einsum(
        "phqk,pkhd->pqhd", weights_low, value_heads, preferred_element_type=jnp.float32
    )
    context = context.reshape(row_count, model_width).astype(jnp.bfloat16)
    attended = jnp.dot(context, out_w, preferred_element_type=jnp.float32) + out_b.astype(
        jnp.float32
    )
    first_out, first_normed, first_inv = layer_norm_parts(
        tok_rows.astype(jnp.float32) + attended,
        ln1_gain.astype(jnp.float32),
        ln1_bias.astype(jnp.float32),
    )
    first_low = first_out.astype(jnp.bfloat16)
    inner_pre = jnp.dot(first_low, ffn_in_w, preferred_element_type=jnp.float32) + ffn_in_b.astype(
        jnp.float32
    )
    act_low = jax.nn.gelu(inner_pre, approximate=False).astype(jnp.bfloat16)
    second = jnp.dot(act_low, ffn_out_w, preferred_element_type=jnp.float32) + ffn_out_b.astype(
        jnp.float32
    )
    final_out, final_normed, final_inv = layer_norm_parts(
        first_low.astype(jnp.float32) + second,
        ln2_gain.astype(jnp.float32),
        ln2_bias.astype(jnp.float32),
    )
    output = final_out.astype(jnp.bfloat16).reshape(page_count, band_rows, model_width)
    grad_final = cotangent.reshape(row_count, model_width).astype(jnp.float32)
    grad_ln2_gain = jnp.sum(grad_final * final_normed, axis=0)
    grad_ln2_bias = jnp.sum(grad_final, axis=0)
    grad_total2 = norm_back(grad_final, final_normed, final_inv, ln2_gain.astype(jnp.float32))
    grad_second_low = grad_total2.astype(jnp.bfloat16)
    grad_ffn_out_b = jnp.sum(grad_second_low, axis=0, dtype=jnp.float32)
    grad_act = jnp.dot(grad_second_low, ffn_out_w.T, preferred_element_type=jnp.float32)
    grad_inner_low = (grad_act * gelu_slope(inner_pre)).astype(jnp.bfloat16)
    grad_ffn_in_b = jnp.sum(grad_inner_low, axis=0, dtype=jnp.float32)
    ffn_share = lax.psum_scatter(
        jnp.concatenate(
            [rows_product(grad_inner_low, first_low), rows_product(act_low, grad_second_low)],
            axis=1,
        ),
        ("band", "page"),
        scatter_dimension=0,
        tiled=True,
    )
    grad_ffn_in_w = ffn_share[:, :model_width].T
    grad_ffn_out_w = ffn_share[:, model_width:]
    grad_first = grad_total2 + jnp.dot(
        grad_inner_low, ffn_in_w.T, preferred_element_type=jnp.float32
    )
    grad_ln1_gain = jnp.sum(grad_first * first_normed, axis=0)
    grad_ln1_bias = jnp.sum(grad_first, axis=0)
    grad_total1 = norm_back(grad_first, first_normed, first_inv, ln1_gain.astype(jnp.float32))
    grad_attn_low = grad_total1.astype(jnp.bfloat16)
    grad_out_b = jnp.sum(grad_attn_low, axis=0, dtype=jnp.float32)
    grad_out_w = rows_product(context, grad_attn_low)
    grad_context = jnp.dot(grad_attn_low, out_w.T, preferred_element_type=jnp.float32).astype(
        jnp.bfloat16
    )
    grad_context = grad_context.reshape(page_count, band_rows, head_count, head_size)
    scores_again = attention_scores(queries, key_heads, families, tables, key_mask, score_scale)
    weights_again = jnp.exp(scores_again - log_total)
    weights_again_low = weights_again.astype(jnp.bfloat16)
    grad_value = jnp.einsum(
        "phqk,pqhd->pkhd", weights_again_low, grad_context, preferred_element_type=jnp.float32
    )
    grad_weights = jnp.einsum(
        "pqhd,pkhd->phqk", grad_context, value_heads, preferred_element_type=jnp.float32
    )
    grad_scores_low = (
        weights_again
        * (grad_weights - jnp.sum(weights_again * grad_weights, axis=-1, keepdims=True))
    ).astype(jnp.bfloat16)
    grad_query = (
        jnp.einsum(
            "phqk,pkhd->pqhd", grad_scores_low, key_heads, preferred_element_type=jnp.float32
        )
        * score_scale
    )
    grad_key = (
        jnp.einsum("phqk,pqhd->pkhd", grad_scores_low, queries, preferred_element_type=jnp.float32)
        * score_scale
    )
    grad_rel_table, grad_x_table, grad_y_table = table_grads(families, tables, grad_scores_low)
    grad_pairs = jnp.concatenate(
        [
            grad_key.reshape(page_count, key_count, model_width),
            grad_value.reshape(page_count, key_count, model_width),
        ],
        axis=-1,
    )
    visual_count = visual_pairs.shape[1]
    back_visual = shifted(grad_pairs[:, :visual_count].astype(jnp.bfloat16), "band", -1).astype(
        jnp.float32
    )
    band_part = grad_pairs[:, visual_count:]
    rim_edges = jnp.concatenate(
        [band_part[:, :HALF], band_part[:, band_part.shape[1] - HALF :]], axis=1
    )
    returned = extended_2(rim_edges.astype(jnp.bfloat16), (("band", 1),), HALF).astype(
        rim_edges.dtype
    )
    own_pairs = band_part[:, HALF : HALF + band_rows]
    own_pairs = own_pairs.at[:, :HALF].add(returned[:, :HALF])
    own_pairs = own_pairs.at[:, band_rows - HALF :].add(returned[:, 3 * HALF :])
    own_pairs = own_pairs.at[:, :visual_count].add(back_visual)
    grad_mixed_low = jnp.concatenate(
        [grad_query.reshape(row_count, model_width), own_pairs.reshape(row_count, 2 * model_width)],
        axis=1,
    ).astype(jnp.bfloat16)
    grad_q_bias = jnp.sum(grad_mixed_low[:, :model_width], axis=0, dtype=jnp.float32)
    grad_v_bias = jnp.sum(grad_mixed_low[:, 2 * model_width :], axis=0, dtype=jnp.float32)
    grad_qkv_w = rows_product(tok_rows, grad_mixed_low)
    grad_hidden = grad_total1 + jnp.dot(grad_mixed_low, qkv_w.T, preferred_element_type=jnp.float32)
    grad_hidden = grad_hidden.reshape(page_count, band_rows, model_width)
    (
        grad_qkv_w,
        grad_q_bias,
        grad_v_bias,
        grad_rel_table,
        grad_x_table,
        grad_y_table,
        grad_out_b,
        grad_ln1_gain,
        grad_ln1_bias,
        grad_ffn_in_b,
        grad_ffn_out_b,
        grad_ln2_gain,
        grad_ln2_bias,
        grad_out_w,
    ) = lax.psum(
        (
            grad_qkv_w,
            grad_q_bias,
            grad_v_bias,
            grad_rel_table,
            grad_x_table,
            grad_y_table,
            grad_out_b,
            grad_ln1_gain,
            grad_ln1_bias,
            grad_ffn_in_b,
            grad_ffn_out_b,
            grad_ln2_gain,
            grad_ln2_bias,
            grad_out_w,
        ),
        ("band", "page"),
    )
    return (
        output,
        grad_hidden,
        grad_qkv_w,
        grad_q_bias,
        grad_v_bias,
        grad_rel_table,
        grad_x_table,
        grad_y_table,
        grad_out_w,
        grad_out_b,
        grad_ln1_gain,
        grad_ln1_bias,
        grad_ffn_in_w,
        grad_ffn_in_b,
        grad_ffn_out_w,
        grad_ffn_out_b,
        grad_ln2_gain,
        grad_ln2_bias,
    )


def solution(mesh):
    in_specs = (
        P("page", "band", None),
        P("page", "band", None),
        P("page"),
        P("page", None),
        P("page", None),
        P(),
        P(),
        P(),
        P(),
        P(),
        P(),
        P(),
        P(),
        P(),
        P(),
        P(),
        P(),
        P(),
        P(),
        P(),
        P(),
    )
    out_specs = (
        P("page", "band", None),
        P("page", "band", None),
        P(),
        P(),
        P(),
        P(),
        P(),
        P(),
        P(),
        P(),
        P(),
        P(),
        P(None, ("band", "page")),
        P(),
        P(("band", "page"), None),
        P(),
        P(),
        P(),
    )
    return jax.shard_map(local, mesh=mesh, in_specs=in_specs, out_specs=out_specs, check_vma=False)
```

profile of v0, /device:TPU:0, one launch (start us, length us, event | category | flops | bytes accessed | tf_op | source)
XLA Modules:
  0.0 870.9 jit_solution(8689713900174890074)
XLA Ops:
  9.2 5.1 add_convert_fusion
  18.9 3.2 collective-permute-start
  34.0 2.7 gather_fusion
  36.8 2.7 gather_fusion.1
  48.3 2.7 convert_reduce_fusion.2
  51.6 3.9 fusion.105
  55.5 21.1 %fusion.1 = f32[3,288,465,12]{2,3,1,0:T(8,128)} fusion(s32[3,288,465]{2,1,0:T(8,128)S(1)} %fusion.105, bf16[64,12]{0,1:T(8,128)(2,1)} %param.39), kind=kOutput, calls=%fused_computation.4 | convolution fusion | flops 642816000 | bytes 20893056 | tf_op jit(solution)/shard_map/pqkc,ch->phqk/dot_general | solution.py:119
  76.7 3.1 fusion.89
  79.9 19.9 %fusion.3 = f32[3,288,465,12]{2,3,1,0:T(8,128)} fusion(s32[3,288,465]{2,1,0:T(8,128)S(1)} %fusion.89, bf16[64,12]{0,1:T(8,128)(2,1)S(1)} %copy-done.36), kind=kOutput, calls=%fused_computation.7 | convolution fusion | flops 642816000 | bytes 20893056 | tf_op jit(solution)/shard_map/pqkc,ch->phqk/dot_general | solution.py:119
  100.8 13.0 %fusion.9 = f32[3,288,465,12]{2,3,1,0:T(8,128)} fusion(s32[288,465]{1,0:T(8,128)S(1)} %fusion.138, bf16[32,12]{0,1:T(8,128)(2,1)S(1)} %copy-done.37), kind=kOutput, calls=%fused_computation.14 | convolution fusion | flops 321408000 | bytes 19820928 | tf_op jit(solution)/shard_map/pqkc,ch->phqk/dot_general | solution.py:119
  114.4 2.5 slice.160
  116.9 5.2 reshape.529
  122.1 6.0 copy.122
  138.3 3.0 bitcast_multiply_fusion.1
  141.3 3.0 pad_maximum_fusion.2
  144.3 2.3 fusion.162
  146.7 4.2 copy.121
  150.9 61.8 %fusion.165 = (f32[3,12,288]{2,1,0:T(8,128)S(1)}, f32[3,12,288,465]{3,2,1,0:T(8,128)}) fusion(f32[3,288,465,12]{2,3,1,0:T(8,128)} %fusion.1, f32[3,288,465,12]{2,3,1,0:T(8,128)} %fusion.3, f32[3,288,465,12]{2,3,1,0:T(8,128)} %fusion.9, bf16[3,288,12,64]{1,3,2,0:T(8,128)(2,1)} %copy.122, bf16[3,465,12,64]{1,3,2,0:T(8,128)(2,1)} %bitcast.98, ...), kind=kOutput, calls=%fused_computation.264 | convolution fusion | flops 646019712 | bytes 81050976 | tf_op jit(solution)/shard_map/pqhd,pkhd->phqk/dot_general | solution.py:145
  212.7 10.3 %exponential_reduce_fusion = f32[3,12,288]{2,1,0:T(8,128)S(1)} fusion(f32[3,12,288,465]{3,2,1,0:T(8,128)} %get-tuple-element.171, f32[3,12,288]{2,1,0:T(8,128)S(1)} %get-tuple-element.170), kind=kLoop, calls=%fused_computation.24 | loop fusion | flops 9631872 | bytes 19367424 | tf_op jit(solution)/shard_map/reduce_sum | solution.py:234
  223.7 4.2 copy.119
  227.9 9.6 %convert_bitcast_fusion = bf16[3,288,12,64]{1,3,2,0:T(8,128)(2,1)S(1)} fusion(bf16[3,465,12,64]{1,3,2,0:T(8,128)(2,1)} %bitcast.100, f32[3,12,288,465]{3,2,1,0:T(8,128)} %get-tuple-element.171, f32[3,12,288]{2,1,0:T(8,128)} %log_add_fusion), kind=kOutput, calls=%fused_computation.165 | convolution fusion | flops 627409152 | bytes 22795776 | tf_op jit(solution)/shard_map/phqk,pkhd->pqhd/dot_general | solution.py:237
  237.5 2.9 copy.130
  240.4 5.3 convert_element_type.396
  245.7 3.6 fusion.166
  250.2 32.0 %fusion.19 = (bf16[864,3072]{1,0:T(8,128)(2,1)S(1)}, f32[864,3072]{1,0:T(8,128)}) fusion(f32[3072]{0:T(1024)S(1)} %copy-done.34, bf16[768,3072]{1,0:T(8,128)(2,1)} %param.44, f32[864,768]{1,0:T(8,128)S(1)} %get-tuple-element.173, f32[768]{0:T(1024)S(1)} %copy-done.38, f32[768]{0:T(1024)S(1)} %copy-done.31, f32[864]{0:T(1024)S(1)} %add_rsqrt_fusion.1, ...), kind=kOutput, calls=%fused_computation.39 | convolution fusion | flops 4255358976 | bytes 23323392 | tf_op jit(solution)/shard_map/dot_general | solution.py:250
  282.3 4.6 fusion.167
  289.7 2.7 convert_reduce_fusion.3
  292.5 11.5 %convert_reduce_fusion = (f32[3072]{0:T(1024)}, bf16[864,3072]{1,0:T(8,128)(2,1)S(1)}) fusion(f32[864,3072]{1,0:T(8,128)} %get-tuple-element.175, f32[3072]{0:T(1024)S(1)} %copy-done.34, bf16[3072,768]{1,0:T(8,128)(2,1)S(1)} %bitcast.112, f32[864,768]{1,0:T(8,128)S(1)} %get-tuple-element.150), kind=kOutput, calls=%fused_computation.46 | convolution fusion | flops 4112028672 | bytes 23322624 | tf_op jit(solution)/shard_map/dot_general | solution.py:269
  304.0 5.5 multiply_reduce_fusion.1
  312.5 2.3 convolution_convert_fusion
  314.8 5.2 reshape.530
  320.1 5.8 copy.132
  325.9 11.7 %fusion.35 = f32[3,12,64,465]{3,2,1,0:T(8,128)} fusion(bf16[3,288,12,64]{1,3,2,0:T(8,128)(2,1)} %copy.132, f32[3,12,288,465]{3,2,1,0:T(8,128)} %get-tuple-element.171, f32[3,12,288]{2,1,0:T(8,128)} %log_add_fusion), kind=kOutput, calls=%fused_computation.69 | convolution fusion | flops 626745600 | bytes 24938496 | tf_op jit(solution)/shard_map/phqk,pqhd->pkhd/dot_general | solution.py:299
  337.6 16.0 %multiply_reduce_fusion = (f32[3,12,288]{2,1,0:T(8,128)}, f32[3,12,288,465]{3,2,1,0:T(8,128)}) fusion(f32[3,12,288,465]{3,2,1,0:T(8,128)} %get-tuple-element.171, f32[3,12,288]{2,1,0:T(8,128)} %log_add_fusion, bf16[3,288,12,64]{1,3,2,0:T(8,128)(2,1)} %copy.132, bf16[3,465,12,64]{1,3,2,0:T(8,128)(2,1)} %bitcast.101), kind=kOutput, calls=%fused_computation.22 | convolution fusion | flops 631556352 | bytes 42121728 | tf_op jit(solution)/shard_map/pqhd,pkhd->phqk/dot_general | solution.py:302
  353.6 14.4 %multiply_convert_fusion = bf16[3,12,288,465]{3,2,1,0:T(8,128)(2,1)S(1)} fusion(f32[3,12,288,465]{3,2,1,0:T(8,128)} %get-tuple-element.180, f32[3,12,288,465]{3,2,1,0:T(8,128)} %get-tuple-element.171, f32[3,12,288]{2,1,0:T(8,128)} %get-tuple-element.179, f32[3,12,288]{2,1,0:T(8,128)} %log_add_fusion), kind=kLoop, calls=%fused_computation.21 | loop fusion | flops 19284480 | bytes 48294144 | tf_op jit(solution)/shard_map/convert_element_type | solution.py:308
  368.0 4.0 copy-done.1
  372.0 3.9 broadcast_multiply_fusion
  375.9 8.5 fusion.109
  384.4 5.9 copy.137
  390.3 6.3 copy.136
  396.6 4.2 fusion.33
  402.0 4.7 collective-permute-start.2
  408.2 2.8 fusion.155
  413.1 2.9 copy.133
  416.0 5.3 reshape.493
  421.3 2.5 copy.138
  423.8 3.2 fusion.34
  430.1 2.4 copy-done.2
  434.6 5.0 scatter-add.14
  439.6 3.0 convert.19
  444.1 6.2 convolution_bitcast_fusion
  450.4 8.4 fusion.158
  458.8 7.9 fusion.168
  466.8 7.1 pad_maximum_fusion
  473.8 18.8 %copy.151 = f32[3072,1536]{1,0:T(8,128)} copy(f32[3072,1536]{0,1:T(8,128)} %pad_maximum_fusion) | data formatting | bytes 37748736
  494.8 25.0 %fusion.117 = f32[64,12]{0,1:T(8,128)} fusion(bf16[3,12,288,465]{3,2,1,0:T(8,128)(2,1)} %copy-done.1, s32[3,288,465]{2,1,0:T(8,128)} %copy-done.14), kind=kOutput, calls=%fused_computation.176 | convolution fusion | flops 642816000 | bytes 11252352 | tf_op jit(solution)/shard_map/phqk,pqkc->ch/dot_general | solution.py:133
  519.8 25.6 %fusion.120 = f32[64,12]{0,1:T(8,128)} fusion(bf16[3,12,288,465]{3,2,1,0:T(8,128)(2,1)} %copy-done.1, s32[3,288,465]{2,1,0:T(8,128)S(1)} %copy-done.13), kind=kOutput, calls=%fused_computation.177 | convolution fusion | flops 642816000 | bytes 11252352 | tf_op jit(solution)/shard_map/phqk,pqkc->ch/dot_general | solution.py:133
  545.5 21.9 %fusion.114 = f32[32,12]{0,1:T(8,128)} fusion(bf16[3,12,288,465]{3,2,1,0:T(8,128)(2,1)S(1)} %bitcast.97, s32[288,465]{1,0:T(8,128)S(1)} %copy-done.7), kind=kOutput, calls=%fused_computation.175 | convolution fusion | flops 321408000 | bytes 10179456 | tf_op jit(solution)/shard_map/phqk,pqkc->ch/dot_general | solution.py:133
  568.3 45.7 %all-reduce = (f32[768]{0:T(1024)}, f32[768]{0:T(1024)}, f32[32,12]{0,1:T(8,128)}, f32[64,12]{0,1:T(8,128)}, f32[64,12]{0,1:T(8,128)}, /*index=5*/f32[768]{0:T(1...) all-reduce(f32[768]{0:T(1024)} %convert_reduce_fusion.1, ...), channel_id=1, replica_groups=mesh['band'=2,'page'=16] {'band','page'}, use_global_device_ids=true, to_apply=%region_14.16 | all-reduce | flops 11136 | bytes 89088 | tf_op jit(solution)/shard_map/psum | solution.py:366
  614.0 7.9 fusion.108
  621.9 25.5 %all-reduce.7.cloned.1.call-done = (f32[768,2304]{0,1:T(8,128)}, f32[768,768]{1,0:T(8,128)}) async-done(((f32[768,2304]{0,1:T(8,128)}, f32[768,768]{1,0:T(8,128)}), (f32[768,2304]{0,1:T(8,128)}, f32[768,768]{1,0:T(8,128)})) %all-reduce.7.cloned.1.call-update) | async-done | bytes 9437200 | tf_op jit(solution)/shard_map/psum | solution.py:366
  647.4 8.0 copy.142
  655.4 203.6 %reduce-scatter.4.cloned.1.call-done = f32[96,1536]{1,0:T(8,128)} async-done(((f32[3072,1536]{1,0:T(8,128)}), f32[96,1536]{1,0:T(8,128)}) %reduce-scatter.4.cloned.1.call-update) | async-done | bytes 589840
  860.9 3.2 copy.185
  (187 shorter events, 63.6 us)
Async XLA Ops:
  7.2 2.0 copy-start
  7.2 134.1 %all-reduce.5.cloned.1.call-start = ((), (), s32[]{:S(2)}) async-start(), calls=%async_computation.1 | async-start | bytes 1032192 | tf_op jit(solution)/shard_map/psum | solution.py:42
  14.4 1.9 copy-start.18
  16.3 1.5 copy-start.5
  18.9 122.4 %collective-permute-start = (bf16[3,64,1536]{2,1,0:T(8,128)(2,1)}, bf16[3,64,1536]{2,1,0:T(8,128)(2,1)}, u32[]{:S(2)}, u32[]{:S(2)}) collective-permute-start(bf16[3,64,1536]{2,1,0:T(8,128)(2,1)} %get-tuple-element.160), channel_id=1, source_target_pairs={{0,16},{1,17},{2,18},{3,19},{4,20},{5,21},{6,22},{7,23},{8,24},{9,... | collective-permute-start | bytes 1769480 | tf_op jit(solution)/shard_map/ppermute | solution.py:31
  22.1 119.3 %collective-permute-start.1 = (bf16[3,64,1536]{2,1,0:T(8,128)(2,1)}, bf16[3,64,1536]{2,1,0:T(8,128)(2,1)}, u32[]{:S(2)}, u32[]{:S(2)}) collective-permute-start(bf16[3,64,1536]{2,1,0:T(8,128)(2,1)} %get-tuple-element.161), channel_id=1, source_target_pairs={{16,0},{17,1},{18,2},{19,3},{20,4},{21,5},{22,6},{23,7},{24,8},{25... | collective-permute-start | bytes 1769480 | tf_op jit(solution)/shard_map/ppermute | solution.py:33
  25.3 622.2 %all-reduce.7.cloned.1.call-start = ((), (), s32[]{:S(2)}) async-start(), calls=%async_computation.3 | async-start | bytes 18874368 | tf_op jit(solution)/shard_map/psum | solution.py:366
  47.6 53.2 %copy-start.6 = (s32[288,465]{1,0:T(8,128)}, s32[288,465]{1,0:T(8,128)S(1)}, u32[]{:S(2)}) copy-start(s32[288,465]{1,0:T(8,128)S(1)} %fusion.138) | copy-start | bytes 1607044
  55.4 21.2 %copy-start.12 = (s32[3,288,465]{2,1,0:T(8,128)}, s32[3,288,465]{2,1,0:T(8,128)S(1)}, u32[]{:S(2)}) copy-start(s32[3,288,465]{2,1,0:T(8,128)S(1)} %fusion.105) | copy-start | bytes 4821124
  55.5 21.2 %copy-start.25 = (s32[3,288]{1,0:T(4,128)S(1)}, s32[3,288]{1,0:T(4,128)}, u32[]{:S(2)}) copy-start(s32[3,288]{1,0:T(4,128)} %get-tuple-element.184) | copy-start | bytes 10372
  55.5 24.3 %copy-start.36 = (bf16[64,12]{0,1:T(8,128)(2,1)S(1)}, bf16[64,12]{0,1:T(8,128)(2,1)}, u32[]{:S(2)}) copy-start(bf16[64,12]{0,1:T(8,128)(2,1)} %param.38) | copy-start | bytes 4612
  79.8 20.0 %copy-start.14 = (s32[3,288,465]{2,1,0:T(8,128)}, s32[3,288,465]{2,1,0:T(8,128)S(1)}, u32[]{:S(2)}) copy-start(s32[3,288,465]{2,1,0:T(8,128)S(1)} %fusion.89) | copy-start | bytes 4821124
  79.8 20.0 %copy-start.26 = (s32[288]{0:T(512)S(1)}, s32[288]{0:T(512)}, u32[]{:S(2)}) copy-start(s32[288]{0:T(512)} %iota_add_fusion) | copy-start | bytes 3460
  79.8 20.0 %copy-start.42 = (pred[465]{0:T(512)(128)(4,1)S(1)}, pred[465]{0:T(512)(128)(4,1)}, u32[]{:S(2)}) copy-start(pred[465]{0:T(512)(128)(4,1)} %get-tuple-element.164) | copy-start | bytes 1399
  79.8 20.0 %copy-start.44 = (pred[288]{0:T(512)(128)(4,1)S(1)}, pred[288]{0:T(512)(128)(4,1)}, u32[]{:S(2)}) copy-start(pred[288]{0:T(512)(128)(4,1)} %broadcast_compare_fusion) | copy-start | bytes 868
  79.9 20.9 %copy-start.37 = (bf16[32,12]{0,1:T(8,128)(2,1)S(1)}, bf16[32,12]{0,1:T(8,128)(2,1)}, u32[]{:S(2)}) copy-start(bf16[32,12]{0,1:T(8,128)(2,1)} %param.37) | copy-start | bytes 2308
  100.7 13.0 %copy-start.43 = (pred[465]{0:T(512)(128)(4,1)S(1)}, pred[465]{0:T(512)(128)(4,1)}, u32[]{:S(2)}) copy-start(pred[465]{0:T(512)(128)(4,1)} %get-tuple-element.153) | copy-start | bytes 1399
  122.1 12.4 %copy-start.24 = (f32[3,288]{1,0:T(4,128)S(1)}, f32[3,288]{1,0:T(4,128)}, u32[]{:S(2)}) copy-start(f32[3,288]{1,0:T(4,128)} %broadcast_multiply_fusion.1) | copy-start | bytes 10372
  122.1 14.3 %copy-start.35 = (pred[3,465]{1,0:T(4,128)(4,1)S(1)}, pred[3,465]{1,0:T(4,128)(4,1)}, u32[]{:S(2)}) copy-start(pred[3,465]{1,0:T(4,128)(4,1)} %compare_and_fusion) | copy-start | bytes 4189
  240.4 5.3 copy-start.41
  245.7 36.5 %slice-start.3 = ((s8[4718592]{0:T(1024)(128)(4,1)}), s8[4194304]{0:T(1024)(128)(4,1)S(1)}, s32[]{:S(2)}) async-start(s8[4718592]{0:T(1024)(128)(4,1)} %bitcast.111), calls=%async_computation.7 | async-start | bytes 8388608
  249.4 60.1 %copy-start.9 = (f32[864,768]{1,0:T(8,128)}, f32[864,768]{1,0:T(8,128)S(1)}, u32[]{:S(2)}) copy-start(f32[864,768]{1,0:T(8,128)S(1)} %get-tuple-element.173) | copy-start | bytes 7962628
  249.4 0.7 copy-start.31
  249.4 0.8 copy-start.34
  249.4 0.8 copy-start.38
  250.2 32.0 %copy-start.40 = (f32[768]{0:T(1024)S(1)}, f32[768]{0:T(1024)}, u32[]{:S(2)}) copy-start(f32[768]{0:T(1024)} %convert_element_type.404) | copy-start | bytes 9220
  250.2 32.0 %slice-start.4 = ((s8[4718592]{0:T(1024)(128)(4,1)}), s8[524288]{0:T(1024)(128)(4,1)S(1)}, s32[]{:S(2)}) async-start(s8[4718592]{0:T(1024)(128)(4,1)} %bitcast.111), calls=%async_computation.8 | async-start | bytes 1048576
  282.2 4.7 copy-start.47
  282.3 5.1 copy-start.11
  286.9 1.3 copy-start.4
  288.2 1.5 copy-start.32
  288.2 1.5 copy-start.33
  289.7 14.2 %slice-start.5 = ((s8[4718592]{0:T(1024)(128)(4,1)}), s8[4194304]{0:T(1024)(128)(4,1)S(1)}, s32[]{:S(2)}) async-start(s8[4718592]{0:T(1024)(128)(4,1)} %bitcast.113), calls=%async_computation.9 | async-start | bytes 8388608
  292.5 11.5 %copy-start.21 = (f32[864,768]{1,0:T(8,128)}, f32[864,768]{1,0:T(8,128)S(1)}, u32[]{:S(2)}) copy-start(f32[864,768]{1,0:T(8,128)S(1)} %get-tuple-element.150) | copy-start | bytes 7962628
  292.5 11.5 %slice-start.6 = ((s8[4718592]{0:T(1024)(128)(4,1)}), s8[524288]{0:T(1024)(128)(4,1)S(1)}, s32[]{:S(2)}) async-start(s8[4718592]{0:T(1024)(128)(4,1)} %bitcast.113), calls=%async_computation.10 | async-start | bytes 1048576
  303.9 5.5 copy-start.48
  309.4 3.1 copy-start.46
  311.0 1.5 copy-start.19
  353.6 18.4 %copy-start.8 = (bf16[3,288,12,64]{1,3,2,0:T(8,128)(2,1)S(1)}, bf16[3,288,12,64]{1,3,2,0:T(8,128)(2,1)}, u32[]{:S(2)}) copy-start(bf16[3,288,12,64]{1,3,2,0:T(8,128)(2,1)} %copy.122) | copy-start | bytes 3981316
  368.0 4.0 copy-start.1
  372.0 3.9 copy-start.3
  396.6 11.6 %copy-start.20 = (f32[864,768]{1,0:T(8,128)S(1)}, f32[864,768]{1,0:T(8,128)}, u32[]{:S(2)}) copy-start(f32[864,768]{1,0:T(8,128)} %copy-done.19) | copy-start | bytes 7962628
  396.6 11.6 %copy-start.22 = (bf16[864,768]{0,1:T(8,128)(2,1)S(1)}, bf16[864,768]{0,1:T(8,128)(2,1)}, u32[]{:S(2)}) copy-start(bf16[864,768]{0,1:T(8,128)(2,1)} %convert_element_type.396) | copy-start | bytes 3981316
  402.0 25.0 %collective-permute-start.2 = (bf16[3,64,1536]{2,1,0:T(8,128)(2,1)}, bf16[3,64,1536]{2,1,0:T(8,128)(2,1)}, u32[]{:S(2)}, u32[]{:S(2)}) collective-permute-start(bf16[3,64,1536]{2,1,0:T(8,128)(2,1)} %get-tuple-element.155), channel_id=1, source_target_pairs={{0,16},{1,17},{2,18},{3,19},{4,20},{5,21},{6,22},{7,23},{8,24},{9,... | collective-permute-start | bytes 1769480 | tf_op jit(solution)/shard_map/ppermute | solution.py:31
  406.7 6.3 copy-start.15
  406.7 20.3 %collective-permute-start.3 = (bf16[3,64,1536]{2,1,0:T(8,128)(2,1)}, bf16[3,64,1536]{2,1,0:T(8,128)(2,1)}, u32[]{:S(2)}, u32[]{:S(2)}) collective-permute-start(bf16[3,64,1536]{2,1,0:T(8,128)(2,1)} %get-tuple-element.156), channel_id=1, source_target_pairs={{16,0},{17,1},{18,2},{19,3},{20,4},{21,5},{22,6},{23,7},{24,8},{25... | collective-permute-start | bytes 1769480 | tf_op jit(solution)/shard_map/ppermute | solution.py:33
  411.8 18.3 %collective-permute-start.4 = (bf16[3,49,1536]{2,1,0:T(8,128)(2,1)}, bf16[3,49,1536]{2,1,0:T(8,128)(2,1)}, u32[]{:S(2)}, u32[]{:S(2)}) collective-permute-start(bf16[3,49,1536]{2,1,0:T(8,128)(2,1)} %slice.170), channel_id=1, source_target_pairs={{16,0},{17,1},{18,2},{19,3},{20,4},{21,5},{22,6},{23,7},{24,8},{25... | collective-permute-start | bytes 1354760 | tf_op jit(solution)/shard_map/ppermute | solution.py:48
  430.0 2.4 copy-start.2
  439.6 4.6 copy-start.23
  439.6 4.6 copy-start.45
  442.5 1.6 copy-start.16
  450.3 8.5 copy-start.39
  450.4 408.6 %reduce-scatter.4.cloned.1.call-start = ((), (), s32[]{:S(2)}) async-start(), calls=%async_computation.2 | async-start | bytes 19464192
  450.4 8.4 copy-start.10
  494.8 25.0 %copy-start.13 = (s32[3,288,465]{2,1,0:T(8,128)S(1)}, s32[3,288,465]{2,1,0:T(8,128)}, u32[]{:S(2)}) copy-start(s32[3,288,465]{2,1,0:T(8,128)} %copy-done.12) | copy-start | bytes 4821124
  494.8 50.6 %slice-start = ((s8[10616832]{0:T(1024)(128)(4,1)}), s8[4194304]{0:T(1024)(128)(4,1)S(1)}, s32[]{:S(2)}) async-start(s8[10616832]{0:T(1024)(128)(4,1)} %bitcast.96), calls=%async_computation.4 | async-start | bytes 8388608
  494.8 50.6 %slice-start.1 = ((s8[10616832]{0:T(1024)(128)(4,1)}), s8[4194304]{0:T(1024)(128)(4,1)S(1)}, s32[]{:S(2)}) async-start(s8[10616832]{0:T(1024)(128)(4,1)} %bitcast.96), calls=%async_computation.5 | async-start | bytes 8388608
  519.8 25.6 %slice-start.2 = ((s8[10616832]{0:T(1024)(128)(4,1)}), s8[2228224]{0:T(1024)(128)(4,1)S(1)}, s32[]{:S(2)}) async-start(s8[10616832]{0:T(1024)(128)(4,1)} %bitcast.96), calls=%async_computation.6 | async-start | bytes 4456448
  519.8 25.6 %copy-start.7 = (s32[288,465]{1,0:T(8,128)S(1)}, s32[288,465]{1,0:T(8,128)}, u32[]{:S(2)}) copy-start(s32[288,465]{1,0:T(8,128)} %copy-done.6) | copy-start | bytes 1607044
  545.4 22.0 %copy-start.17 = (bf16[3,288,1536]{2,1,0:T(8,128)(2,1)S(1)}, bf16[3,288,1536]{2,1,0:T(8,128)(2,1)}, u32[]{:S(2)}) copy-start(bf16[3,288,1536]{2,1,0:T(8,128)(2,1)} %copy-done.16) | copy-start | bytes 7962628
  545.4 22.8 %copy-start.27 = (f32[768]{0:T(1024)S(1)}, f32[768]{0:T(1024)}, u32[]{:S(2)}) copy-start(f32[768]{0:T(1024)} %get-tuple-element.133) | copy-start | bytes 9220
  545.4 22.8 %copy-start.28 = (f32[768]{0:T(1024)S(1)}, f32[768]{0:T(1024)}, u32[]{:S(2)}) copy-start(f32[768]{0:T(1024)} %get-tuple-element.129) | copy-start | bytes 9220
  545.5 22.8 %copy-start.29 = (f32[768]{0:T(1024)S(1)}, f32[768]{0:T(1024)}, u32[]{:S(2)}) copy-start(f32[768]{0:T(1024)} %get-tuple-element.149) | copy-start | bytes 9220
  545.5 22.8 %copy-start.30 = (f32[768]{0:T(1024)S(1)}, f32[768]{0:T(1024)}, u32[]{:S(2)}) copy-start(f32[768]{0:T(1024)} %get-tuple-element.151) | copy-start | bytes 9220
Sparse Core Ops, SparseCore 0:
  25.4 22.3 all-reduce.4
  450.5 196.9 all-reduce.6
  653.9 205.0 reduce-scatter.3
where the time goes:
time: 876 us; the launch traced here: 871 us
  matrix products  336 us (38%)
  waiting for transfers between devices  229 us (26%)
  local copies, waits for them, and re-layouts  134 us (15%)
  other arithmetic  99.3 us (11%)
  blocking collectives  45.7 us (5%)
  between operations  14.8 us (2%)
  starting transfers between devices  12.3 us (1%)
    unnamed x4, waiting for transfers between devices  204 us
    dot_general x3, matrix products, table_grads(): jnp.einsum('phqk,pqkc->ch', grad_scores_low, one_hots(bucket_ids, table.s...  72.5 us
    dot_general x1, matrix products, attention_scores(): jnp.einsum('pqhd,pkhd->phqk', queries, key_heads, preferred_element_type=...  61.8 us
    dot_general x3, matrix products, score_bias(): jnp.einsum('pqkc,ch->phqk', one_hots(bucket_ids, table.shape[0]), table,...  54.1 us
    psum x1, blocking collectives, local(): lax.psum((grad_qkv_w, grad_q_bias, grad_v_bias, grad_rel_table, grad_x_ta...  45.7 us
    unnamed x115, local copies, waits for them, and re-layouts  44.2 us
    dot_general x1, matrix products, local(): jnp.dot(first_low, ffn_in_w, preferred_element_type=jnp.float32)  32 us
    psum x1, waiting for transfers between devices, local(): lax.psum((grad_qkv_w, grad_q_bias, grad_v_bias, grad_rel_table, grad_x_ta...  25.5 us
  transfers between devices with their start and end apart: 8, of which 2 were waited for; matrix products, arithmetic and copies ran while one was open for 31% of the time, Pallas kernels for 0%

commit v1 on v0

v1 whole, which is shorter than its diff:
```python
import functools
import math

import jax
import jax.numpy as jnp
import numpy as np
from jax import lax
from jax.experimental import pallas as pl
from jax.experimental.pallas import tpu as pltpu
from jax.sharding import PartitionSpec as P

F32 = jnp.float32
BF16 = jnp.bfloat16
I32 = jnp.int32

HEADS = 12
WIDTH = 768
FF = 3072
REL_BUCKETS = 32
REL_REACH = 128
XY_BUCKETS = 64
XY_REACH = 256
VIS = 49
HALF = 64
ROWS = 64
KEYS = 256
CLASSES = 128
HIDE = 127
EPSILON = 1e-05
MASKED = -1e30
NT = (((1,), (1,)), ((), ()))
TN = (((0,), (0,)), ((), ()))
NN = (((1,), (0,)), ((), ()))


def dot(a, b, dims=NN):
    return lax.dot_general(a, b, dims, preferred_element_type=F32)


def bucket_edges(buckets, reach):
    exact = buckets // 4
    spread = buckets // 2 - exact
    return [
        int(np.ceil(exact * (reach / exact) ** (level / spread) - 1e-09))
        for level in range(1, spread)
    ]


def bucket(offsets, buckets, reach):
    distance = jnp.abs(offsets)
    result = jnp.minimum(distance, float(buckets // 4))
    for edge in bucket_edges(buckets, reach):
        result = result + jnp.where(distance >= float(edge), 1.0, 0.0)
    return result + jnp.where(offsets > 0.0, float(buckets // 2), 0.0)


def iota(shape, axis):
    return lax.broadcasted_iota(I32, shape, axis)


def seventh(index):
    return lax.shift_right_logical(index * 37, 8)


def column_of(row):
    size = row.shape[1]
    shape = (size, size)
    spread = jnp.broadcast_to(row, shape)
    return jnp.sum(jnp.where(iota(shape, 0) == iota(shape, 1), spread, 0.0), axis=1, keepdims=True)


def stage_geometry(first_pos, band, x_own, line_own, kx_ref, kc_ref, blocks):
    extent = ROWS * blocks + 2 * HALF
    seq = x_own.shape[-1]
    half_seq = seq // 2

    def window(row):
        left = jnp.concatenate([jnp.zeros((1, HALF), I32), row[:, : extent - HALF]], axis=1)
        start = half_seq - HALF
        right = jnp.concatenate(
            [row[:, start:], jnp.zeros((1, extent - (seq - start)), I32)], axis=1
        )
        return jnp.where(band == 0, left, right)

    pos = first_pos - HALF + iota((1, extent), 1)
    visual = (pos >= 0) & (pos < VIS)
    seventh_pos = seventh(pos)
    x_row = jnp.where(visual, (pos - 7 * seventh_pos) * 142 + 71, window(x_own))
    c_row = jnp.where(visual, 64 + seventh_pos, window(line_own))
    lane = iota((1, HALF), 1)
    x_vis = (lane - 7 * seventh(lane)) * 142 + 71
    c_vis = 64 + seventh(lane)
    for i in range(blocks):
        cut = slice(ROWS * i, ROWS * i + 3 * HALF)
        kx_ref[i : i + 1, :] = jnp.concatenate([x_vis, x_row[:, cut]], axis=1).astype(F32)
        kc_ref[i : i + 1, :] = jnp.concatenate([c_vis, c_row[:, cut]], axis=1).astype(F32)


def key_positions(first_pos, i, shape):
    lane = iota(shape, 1)
    return jnp.where(
        lane < HALF,
        jnp.where(lane < VIS, lane, -1),
        first_pos + ROWS * i - 2 * HALF + lane,
    )


def allowed(first_pos, i, length):
    shape = (ROWS, KEYS)
    lane = iota(shape, 1)
    key = key_positions(first_pos, i, shape)
    query = first_pos + ROWS * i + iota(shape, 0)
    near = (key >= VIS) & (query >= VIS) & (jnp.abs(query - key) <= HALF)
    return (key >= 0) & (key < VIS + length) & ((lane < HALF) | near)


def rel_buckets(first_pos, i):
    shape = (ROWS, KEYS)
    key = key_positions(first_pos, i, shape)
    query = first_pos + ROWS * i + iota(shape, 0)
    return bucket((key - query).astype(F32), REL_BUCKETS, REL_REACH)


def class_y(index):
    return jnp.where(index < 64, 15 * index, 142 * (index - 64) + 71).astype(F32)


def lookup(table_row, index):
    shape = index.shape
    row = jnp.broadcast_to(table_row, (shape[0], 128))
    cuts = [
        jnp.take_along_axis(row, index[:, s : s + 128], axis=1) for s in range(0, shape[1], 128)
    ]
    return cuts[0] if len(cuts) == 1 else jnp.concatenate(cuts, axis=1)


def head_split(tile):
    low = iota(tile.shape, 1) < 64
    zero = jnp.zeros_like(tile)
    return jnp.concatenate([jnp.where(low, tile, zero), jnp.where(low, zero, tile)], axis=0)


def head_join(stack):
    rows = stack.shape[0] // 2
    low = iota((rows, stack.shape[1]), 1) < 64
    return jnp.where(low, stack[:rows], stack[rows:])


def key_tile(kv_ref, i, column):
    return jnp.concatenate(
        [
            kv_ref[0, 0:HALF, column : column + 128],
            kv_ref[0, pl.ds(pl.multiple_of(HALF + ROWS * i, ROWS), 3 * HALF), column : column + 128],
        ],
        axis=0,
    )


def attention_kernel(
    band_ref, len_ref, hid_ref, got_ref, x_ref, line_ref, w_ref, qb_ref, vb_ref,
    rel_ref, xt_ref, yt_ref,
    ctx_ref, p_ref, q_ref, kv_ref, ext_ref,
    kx_ref, kc_ref, rb_ref, yb_ref, ctx_s, tab_ref,
):
    page = pl.program_id(0)
    band = band_ref[0]
    rows = hid_ref.shape[1]
    blocks = q_ref.shape[1] // ROWS
    first_pos = band * rows

    @pl.when(page == 0)
    def _():
        for slot, table in enumerate((rel_ref, xt_ref, yt_ref)):
            count = table.shape[0]
            eye = jnp.where(iota((count, 128), 0) == iota((count, 128), 1), 1.0, 0.0).astype(BF16)
            turned = dot(table[...], eye, TN)
            if slot == 1:
                turned = jnp.where(iota((HEADS, 128), 1) == HIDE, MASKED, turned)
            tab_ref[:HEADS, 128 * slot : 128 * slot + 128] = turned
        for i in range(blocks):
            index = rel_buckets(first_pos, i).astype(I32)
            for h in range(HEADS):
                rb_ref[i, ROWS * h : ROWS * h + ROWS, :] = lookup(tab_ref[h : h + 1, 0:128], index)
        square = (CLASSES, CLASSES)
        gap = class_y(iota(square, 1)) - class_y(iota(square, 0))
        index = jnp.minimum(bucket(gap, XY_BUCKETS, XY_REACH), 63.0).astype(I32)
        for h in range(HEADS):
            yb_ref[:, CLASSES * h : CLASSES * h + CLASSES] = lookup(
                tab_ref[h : h + 1, 256:384], index
            ).astype(BF16)

    own = pl.ds(page, 1)
    stage_geometry(first_pos, band, x_ref[own, :], line_ref[own, :], kx_ref, kc_ref, blocks)
    ext_ref[0, :HALF] = jnp.where(band == 0, hid_ref[0, :HALF], got_ref[0, :HALF])
    ext_ref[0, HALF : 2 * HALF] = got_ref[0, HALF:]
    ext_ref[0, 2 * HALF :] = hid_ref[0]
    q_ref[0, 0:rows] = (
        (dot(hid_ref[0], w_ref[:, :WIDTH]) + qb_ref[...].astype(F32)).astype(BF16).astype(F32)
        * 0.125
    ).astype(BF16)
    q_ref[0, rows:] = jnp.zeros((q_ref.shape[1] - rows, WIDTH), BF16)
    kv_ref[0, : 2 * HALF + rows, :WIDTH] = dot(ext_ref[0], w_ref[:, WIDTH : 2 * WIDTH]).astype(BF16)
    kv_ref[0, : 2 * HALF + rows, WIDTH:] = (
        dot(ext_ref[0], w_ref[:, 2 * WIDTH :]) + vb_ref[...].astype(F32)
    ).astype(BF16)
    kv_ref[0, 2 * HALF + rows : 3 * HALF + rows] = kv_ref[0, HALF : 2 * HALF]
    tail = kv_ref.shape[1] - (3 * HALF + rows)
    kv_ref[0, 3 * HALF + rows :] = jnp.zeros((tail, 2 * WIDTH), BF16)

    def block(i, _):
        start = pl.multiple_of(ROWS * i, ROWS)
        kx = kx_ref[pl.ds(i, 1), :]
        kc = kc_ref[pl.ds(i, 1), :]
        gap = kx - column_of(kx[:, 2 * HALF : 3 * HALF])
        index = jnp.where(
            allowed(first_pos, i, len_ref[page]), bucket(gap, XY_BUCKETS, XY_REACH), float(HIDE)
        ).astype(I32)
        pick_q = jnp.where(
            iota((ROWS, CLASSES), 1).astype(F32) == column_of(kc[:, 2 * HALF : 3 * HALF]), 1.0, 0.0
        ).astype(BF16)
        pick_k = jnp.where(
            iota((KEYS, CLASSES), 1).astype(F32) == column_of(kc), 1.0, 0.0
        ).astype(BF16)
        pairs = range(HEADS // 2)
        scores = []
        for j in pairs:
            column = 128 * j
            queries = head_split(q_ref[0, pl.ds(start, ROWS), column : column + 128])
            picked = dot(pick_q, yb_ref[:, 2 * column : 2 * column + 256]).astype(BF16)
            picked = jnp.concatenate([picked[:, :128], picked[:, 128:]], axis=0)
            scores.append(
                dot(
                    jnp.concatenate([queries, picked], axis=1),
                    jnp.concatenate([key_tile(kv_ref, i, column), pick_k], axis=1),
                    NT,
                )
            )
        weights = []
        for j in pairs:
            x_bias = jnp.concatenate(
                [lookup(tab_ref[2 * j + e : 2 * j + e + 1, 128:256], index) for e in (0, 1)], axis=0
            )
            biased = scores[j] + rb_ref[i, 128 * j : 128 * j + 128, :] + x_bias
            peak = jnp.max(biased, axis=1, keepdims=True)
            raised = jnp.exp(biased - peak)
            weights.append(
                (raised * (1.0 / jnp.sum(raised, axis=1, keepdims=True))).astype(BF16)
            )
        contexts = [
            dot(weights[j], key_tile(kv_ref, i, WIDTH + 128 * j)) for j in pairs
        ]
        for j in pairs:
            p_ref[0, i, 128 * j : 128 * j + 128, :] = weights[j]
        ctx_s[pl.ds(start, ROWS), :] = jnp.concatenate(
            [head_join(c).astype(BF16) for c in contexts], axis=1
        )
        return 0

    lax.fori_loop(0, blocks, block, 0)
    ctx_ref[0] = ctx_s[:rows]


def page_block(*shape):
    return pl.BlockSpec((1,) + shape, lambda p, *_: (p,) + (0,) * len(shape))


def whole(*shape):
    return pl.BlockSpec(shape, lambda *_: (0,) * len(shape))


def attention_forward(
    band, lengths, hidden, got, x_coord, line_ids, qkv_w, q_bias, v_bias, tables
):
    pages, rows, width = hidden.shape
    blocks = -(-rows // ROWS)
    padded = blocks * ROWS
    ext = padded + 3 * HALF
    shape = jax.ShapeDtypeStruct
    return pl.pallas_call(
        attention_kernel,
        out_shape=(
            shape((pages, rows, width), BF16),
            shape((pages, blocks, HEADS * ROWS, KEYS), BF16),
            shape((pages, padded, width), BF16),
            shape((pages, ext, 2 * width), BF16),
            shape((pages, rows + 2 * HALF, width), BF16),
        ),
        grid_spec=pltpu.PrefetchScalarGridSpec(
            num_scalar_prefetch=2,
            grid=(pages,),
            in_specs=[
                page_block(rows, width),
                page_block(2 * HALF, width),
                whole(*x_coord.shape),
                whole(*line_ids.shape),
                whole(width, 3 * width),
                whole(1, width),
                whole(1, width),
            ]
            + [whole(*table.shape) for table in tables],
            out_specs=[
                page_block(rows, width),
                page_block(blocks, HEADS * ROWS, KEYS),
                page_block(padded, width),
                page_block(ext, 2 * width),
                page_block(rows + 2 * HALF, width),
            ],
            scratch_shapes=[
                pltpu.VMEM((8, KEYS), F32),
                pltpu.VMEM((8, KEYS), F32),
                pltpu.VMEM((blocks, HEADS * ROWS, KEYS), F32),
                pltpu.VMEM((CLASSES, HEADS * CLASSES), BF16),
                pltpu.VMEM((padded, width), BF16),
                pltpu.VMEM((16, 384), F32),
            ],
        ),
        compiler_params=pltpu.CompilerParams(vmem_limit_bytes=56 << 20),
        cost_estimate=pl.CostEstimate(
            flops=2 * pages * (rows + 2 * HALF) * width * 3 * width
            + 8 * pages * padded * HEADS * KEYS * 128,
            bytes_accessed=30 << 20,
            transcendentals=pages * padded * HEADS * KEYS,
        ),
        name="attention_forward",
    )(
        band, lengths, hidden, got, x_coord, line_ids, qkv_w,
        q_bias.reshape(1, width), v_bias.reshape(1, width), *tables,
    )


def layer_norm(total):
    centred = total - jnp.mean(total, axis=1, keepdims=True)
    inverse = lax.rsqrt(jnp.mean(centred * centred, axis=1, keepdims=True) + EPSILON)
    return centred * inverse, inverse


def norm_back(grad, normed, inverse, gain):
    scaled = grad * gain
    return inverse * (
        scaled
        - jnp.mean(scaled, axis=1, keepdims=True)
        - normed * jnp.mean(scaled * normed, axis=1, keepdims=True)
    )


def gelu_parts(inner):
    size = jnp.abs(inner)
    falling = jnp.exp(inner * inner * -0.5)
    t = 1.0 / (1.0 + (0.3275911 * math.sqrt(0.5)) * size)
    poly = 1.061405429 * t - 1.453152027
    poly = poly * t + 1.421413741
    poly = poly * t - 0.284496736
    poly = poly * t + 0.254829592
    tail = (0.5 * poly) * (t * falling)
    share = jnp.where(inner >= 0.0, 1.0 - tail, tail)
    return inner * share, share + inner * falling * (2.0 * math.pi) ** (-0.5)


def column_sum(values):
    return jnp.sum(values, axis=0, keepdims=True)


def accumulate(ref, row, value):
    first = pl.program_id(0) == 0

    @pl.when(first)
    def _():
        ref[row : row + 1, :] = value

    @pl.when(jnp.logical_not(first))
    def _():
        ref[row : row + 1, :] = ref[row : row + 1, :] + value


def ffn_forward_kernel(
    ctx_ref, hid_ref, cot_ref, ob_ref, g1_ref, b1_ref, fb_ref, g2_ref, b2_ref, bin_ref,
    wo_ref, w1_ref, w2_ref,
    out_ref, first_ref, norm_ref, inv_ref, act_ref, slope_ref, dh_ref, ds_ref, sums_ref,
):
    out_b, gain1, bias1, ffn_b, gain2, bias2 = (
        r[...].astype(F32) for r in (ob_ref, g1_ref, b1_ref, fb_ref, g2_ref, b2_ref)
    )
    attended = dot(ctx_ref[0], wo_ref[...]) + out_b
    normed, inverse = layer_norm(hid_ref[0].astype(F32) + attended)
    first = (normed * gain1 + bias1).astype(BF16)
    first_ref[0] = first
    norm_ref[0] = normed
    inv_ref[0] = jnp.broadcast_to(inverse, inv_ref.shape[1:])
    chunk = 768
    count = FF // chunk
    second = first.astype(F32) + ffn_b

    def inner_of(c):
        cut = slice(chunk * c, chunk * c + chunk)
        return dot(first, w1_ref[:, cut]) + bin_ref[:, cut].astype(F32)

    ahead = inner_of(0)
    for c in range(count):
        cut = slice(chunk * c, chunk * c + chunk)
        inner = ahead
        if c + 1 < count:
            ahead = inner_of(c + 1)
        act, slope = gelu_parts(inner)
        act = act.astype(BF16)
        act_ref[0, :, cut] = act
        slope_ref[0, :, cut] = slope.astype(BF16)
        second = second + dot(act, w2_ref[cut, :])
    normed2, inverse2 = layer_norm(second)
    out_ref[0] = (normed2 * gain2 + bias2).astype(BF16)
    grad = cot_ref[0].astype(F32)
    back = norm_back(grad, normed2, inverse2, gain2)
    low = back.astype(BF16)
    dh_ref[0] = back
    ds_ref[0] = low
    accumulate(sums_ref, 0, column_sum(grad * normed2))
    accumulate(sums_ref, 1, column_sum(grad))
    accumulate(sums_ref, 2, column_sum(low.astype(F32)))


def ffn_forward(context, hidden, cotangent, vectors, ffn_in_b, out_w, ffn_in_w, ffn_out_w):
    pages, rows, width = context.shape
    shape = jax.ShapeDtypeStruct
    return pl.pallas_call(
        ffn_forward_kernel,
        out_shape=(
            shape((pages, rows, width), BF16),
            shape((pages, rows, width), BF16),
            shape((pages, rows, width), F32),
            shape((pages, rows, 128), F32),
            shape((pages, rows, FF), BF16),
            shape((pages, rows, FF), BF16),
            shape((pages, rows, width), F32),
            shape((pages, rows, width), BF16),
            shape((8, width), F32),
        ),
        grid=(pages,),
        in_specs=[
            page_block(rows, width),
            page_block(rows, width),
            page_block(rows, width),
        ]
        + [whole(1, width)] * 6
        + [
            whole(1, FF),
            whole(width, width),
            whole(width, FF),
            whole(FF, width),
        ],
        out_specs=[
            page_block(rows, width),
            page_block(rows, width),
            page_block(rows, width),
            page_block(rows, 128),
            page_block(rows, FF),
            page_block(rows, FF),
            page_block(rows, width),
            page_block(rows, width),
            whole(8, width),
        ],
        compiler_params=pltpu.CompilerParams(vmem_limit_bytes=60 << 20),
        cost_estimate=pl.CostEstimate(
            flops=2 * pages * rows * width * (2 * FF + width),
            bytes_accessed=40 << 20,
            transcendentals=pages * rows * FF,
        ),
        name="ffn_forward",
    )(
        context, hidden, cotangent, *[v.reshape(1, width) for v in vectors],
        ffn_in_b.reshape(1, FF), out_w, ffn_in_w, ffn_out_w,
    )


def ffn_backward_kernel(
    ds_ref, slope_ref, dh_ref, norm_ref, inv_ref, g1_ref, wo_ref, w1_ref, w2_ref,
    di_ref, dh1_ref, da_ref, dc_ref, sums_ref, bsum_ref,
):
    low = ds_ref[0]
    chunk = 768
    count = FF // chunk
    total = dh_ref[0]

    def act_of(c):
        return dot(low, w2_ref[chunk * c : chunk * c + chunk, :], NT)

    ahead = act_of(0)
    for c in range(count):
        cut = slice(chunk * c, chunk * c + chunk)
        grad = ahead
        if c + 1 < count:
            ahead = act_of(c + 1)
        inner = (grad * slope_ref[0, :, cut].astype(F32)).astype(BF16)
        di_ref[0, :, cut] = inner
        accumulate(bsum_ref.at[:, cut], 0, column_sum(inner.astype(F32)))
        total = total + dot(inner, w1_ref[:, cut], NT)
    normed = norm_ref[0]
    back = norm_back(total, normed, inv_ref[0, :, 0:1], g1_ref[...].astype(F32))
    low = back.astype(BF16)
    dh1_ref[0] = back
    da_ref[0] = low
    dc_ref[0] = dot(low, wo_ref[...], NT).astype(BF16)
    accumulate(sums_ref, 0, column_sum(total * normed))
    accumulate(sums_ref, 1, column_sum(total))
    accumulate(sums_ref, 2, column_sum(low.astype(F32)))


def ffn_backward(second_low, slope, grad_total, normed, inverse, gain, out_w, ffn_in_w, ffn_out_w):
    pages, rows, width = second_low.shape
    shape = jax.ShapeDtypeStruct
    return pl.pallas_call(
        ffn_backward_kernel,
        out_shape=(
            shape((pages, rows, FF), BF16),
            shape((pages, rows, width), F32),
            shape((pages, rows, width), BF16),
            shape((pages, rows, width), BF16),
            shape((8, width), F32),
            shape((8, FF), F32),
        ),
        grid=(pages,),
        in_specs=[
            page_block(rows, width),
            page_block(rows, FF),
            page_block(rows, width),
            page_block(rows, width),
            page_block(rows, 128),
            whole(1, width),
            whole(width, width),
            whole(width, FF),
            whole(FF, width),
        ],
        out_specs=[
            page_block(rows, FF),
            page_block(rows, width),
            page_block(rows, width),
            page_block(rows, width),
            whole(8, width),
            whole(8, FF),
        ],
        compiler_params=pltpu.CompilerParams(vmem_limit_bytes=60 << 20),
        cost_estimate=pl.CostEstimate(
            flops=2 * pages * rows * width * (2 * FF + width),
            bytes_accessed=40 << 20,
            transcendentals=0,
        ),
        name="ffn_backward",
    )(
        second_low, slope, grad_total, normed, inverse, gain.reshape(1, width),
        out_w, ffn_in_w, ffn_out_w,
    )


def attention_back_kernel(
    p_ref, q_ref, kv_ref, dc_ref,
    dm_ref, ds_ref,
    dkv_ref, dc_s, dq_s,
):
    rows = dc_ref.shape[1]
    blocks = q_ref.shape[1] // ROWS
    dkv_ref[...] = jnp.zeros_like(dkv_ref)
    dc_s[:rows] = dc_ref[0]
    dc_s[rows:] = jnp.zeros((dc_s.shape[0] - rows, WIDTH), BF16)
    def block(i, _):
        start = pl.multiple_of(ROWS * i, ROWS)
        window = pl.ds(pl.multiple_of(HALF + ROWS * i, ROWS), 3 * HALF)
        pairs = range(HEADS // 2)
        grads = []
        for j in pairs:
            column = 128 * j
            grads.append(head_split(dc_s[pl.ds(start, ROWS), column : column + 128]))
        dprobs = [dot(grads[j], key_tile(kv_ref, i, WIDTH + 128 * j), NT) for j in pairs]
        for j in pairs:
            dv = dot(p_ref[0, i, 128 * j : 128 * j + 128, :], grads[j], TN)
            column = WIDTH + 128 * j
            cut = slice(column, column + 128)
            dkv_ref[0:HALF, cut] = dkv_ref[0:HALF, cut] + dv[:HALF]
            dkv_ref[window, cut] = dkv_ref[window, cut] + dv[HALF:]
        lows = []
        for j in pairs:
            probs = p_ref[0, i, 128 * j : 128 * j + 128, :].astype(F32)
            grad = probs * (
                dprobs[j] - jnp.sum(probs * dprobs[j], axis=1, keepdims=True)
            )
            lows.append(grad.astype(BF16))
        dq = [head_join(dot(lows[j], key_tile(kv_ref, i, 128 * j))) for j in pairs]
        dq_s[pl.ds(start, ROWS), :] = (jnp.concatenate(dq, axis=1) * 0.125).astype(BF16)
        for j in pairs:
            cut = slice(128 * j, 128 * j + 128)
            dk = dot(lows[j], head_split(q_ref[0, pl.ds(start, ROWS), cut]), TN)
            dkv_ref[0:HALF, cut] = dkv_ref[0:HALF, cut] + dk[:HALF]
            dkv_ref[window, cut] = dkv_ref[window, cut] + dk[HALF:]

        for j in pairs:
            ds_ref[0, i, 128 * j : 128 * j + 128, :] = lows[j]
        return 0

    lax.fori_loop(0, blocks, block, 0)
    dm_ref[0, : 2 * HALF, :WIDTH] = jnp.zeros((2 * HALF, WIDTH), BF16)
    dm_ref[0, 2 * HALF :, :WIDTH] = dq_s[:rows]
    dm_ref[0, :HALF, WIDTH:] = dkv_ref[:HALF].astype(BF16)
    dm_ref[0, HALF : 2 * HALF, WIDTH:] = (
        dkv_ref[HALF : 2 * HALF] + dkv_ref[2 * HALF + rows : 3 * HALF + rows]
    ).astype(BF16)
    dm_ref[0, 2 * HALF :, WIDTH:] = dkv_ref[2 * HALF : 2 * HALF + rows].astype(BF16)


def attention_backward(probs, queries, pairs, grad_context):
    pages, rows, width = grad_context.shape
    padded = queries.shape[1]
    blocks = padded // ROWS
    ext = pairs.shape[1]
    shape = jax.ShapeDtypeStruct
    return pl.pallas_call(
        attention_back_kernel,
        out_shape=(
            shape((pages, rows + 2 * HALF, 3 * width), BF16),
            shape(probs.shape, BF16),
        ),
        grid=(pages,),
        in_specs=[
            page_block(blocks, HEADS * ROWS, KEYS),
            page_block(padded, width),
            page_block(ext, 2 * width),
            page_block(rows, width),
        ],
        out_specs=[page_block(rows + 2 * HALF, 3 * width), page_block(blocks, HEADS * ROWS, KEYS)],
        scratch_shapes=[
            pltpu.VMEM((ext, 2 * width), F32),
            pltpu.VMEM((padded, width), BF16),
            pltpu.VMEM((padded, width), BF16),
        ],
        compiler_params=pltpu.CompilerParams(vmem_limit_bytes=56 << 20),
        cost_estimate=pl.CostEstimate(
            flops=10 * pages * padded * HEADS * KEYS * 128, bytes_accessed=30 << 20, transcendentals=0
        ),
        name="attention_backward",
    )(probs, queries, pairs, grad_context)


def table_kernel(
    band_ref, ds_ref, x_ref, line_ref, tab_ref, kx_ref, kc_ref, left_ref, right_ref, index_ref
):
    page = pl.program_id(0)
    band = band_ref[0]
    blocks = ds_ref.shape[1]
    first_pos = band * (x_ref.shape[-1] // 2)
    own_page = pl.ds(page, 1)
    stage_geometry(first_pos, band, x_ref[own_page, :], line_ref[own_page, :], kx_ref, kc_ref, blocks)
    slots = iota((REL_BUCKETS + 2 * XY_BUCKETS, KEYS), 0).astype(F32).astype(BF16)
    one = jnp.ones((), BF16)
    zero = jnp.zeros((), BF16)

    def block(i, table_sum):
        left_ref[...] = ds_ref[0, i, :, :128].astype(F32)
        right_ref[...] = ds_ref[0, i, :, 128:].astype(F32)
        kx = kx_ref[pl.ds(i, 1), :]
        ky = class_y(kc_ref[pl.ds(i, 1), :].astype(I32))
        index_ref[0:ROWS] = bucket(kx - column_of(kx[:, 2 * HALF : 3 * HALF]), XY_BUCKETS, XY_REACH)
        index_ref[ROWS : 2 * ROWS] = 64.0 + bucket(
            ky - column_of(ky[:, 2 * HALF : 3 * HALF]), XY_BUCKETS, XY_REACH
        )
        index_ref[2 * ROWS : 3 * ROWS] = 128.0 + rel_buckets(first_pos, i)

        def table_row(q, acc):
            own = jnp.concatenate(
                [
                    jnp.broadcast_to(index_ref[pl.ds(q, 1), :], (XY_BUCKETS, KEYS)),
                    jnp.broadcast_to(index_ref[pl.ds(ROWS + q, 1), :], (XY_BUCKETS, KEYS)),
                    jnp.broadcast_to(index_ref[pl.ds(2 * ROWS + q, 1), :], (REL_BUCKETS, KEYS)),
                ],
                axis=0,
            ).astype(BF16)
            heads = jnp.concatenate(
                [
                    left_ref[pl.ds(q, HEADS, stride=ROWS), :],
                    right_ref[pl.ds(q, HEADS, stride=ROWS), :],
                ],
                axis=1,
            ).astype(BF16)
            return acc + dot(heads, jnp.where(slots == own, one, zero), NT)

        return lax.fori_loop(0, ROWS, table_row, table_sum, unroll=8)

    table_sum = lax.fori_loop(
        0, blocks, block, jnp.zeros((HEADS, REL_BUCKETS + 2 * XY_BUCKETS), F32)
    )

    @pl.when(page == 0)
    def _():
        tab_ref[...] = table_sum

    @pl.when(page > 0)
    def _():
        tab_ref[...] = tab_ref[...] + table_sum


def table_sums(band, grad_scores, x_coord, line_ids):
    pages, blocks, height, keys = grad_scores.shape
    buckets = REL_BUCKETS + 2 * XY_BUCKETS
    return pl.pallas_call(
        table_kernel,
        out_shape=jax.ShapeDtypeStruct((HEADS, buckets), F32),
        grid_spec=pltpu.PrefetchScalarGridSpec(
            num_scalar_prefetch=1,
            grid=(pages,),
            in_specs=[
                page_block(blocks, height, keys),
                whole(*x_coord.shape),
                whole(*line_ids.shape),
            ],
            out_specs=whole(HEADS, buckets),
            scratch_shapes=[
                pltpu.VMEM((8, KEYS), F32),
                pltpu.VMEM((8, KEYS), F32),
                pltpu.VMEM((height, 128), F32),
                pltpu.VMEM((height, 128), F32),
                pltpu.VMEM((3 * ROWS, KEYS), F32),
            ],
        ),
        compiler_params=pltpu.CompilerParams(vmem_limit_bytes=24 << 20),
        cost_estimate=pl.CostEstimate(
            flops=60 * pages * blocks * height * keys * 32, bytes_accessed=6 << 20, transcendentals=0
        ),
        name="table_sums",
    )(band, grad_scores, x_coord, line_ids)


def hidden_back_kernel(dm_ref, dh_ref, w_ref, own_ref, far_ref, sums_ref):
    accumulate(sums_ref, 0, column_sum(dm_ref[0].astype(F32)))
    own_ref[0] = dh_ref[0] + dot(dm_ref[0, 2 * HALF :], w_ref[...], NT)
    far_ref[0] = dot(dm_ref[0, : 2 * HALF, WIDTH:], w_ref[:, WIDTH:], NT).astype(BF16)


def hidden_backward(grad_mixed, grad_total, qkv_w):
    pages, rows, width = grad_total.shape
    shape = jax.ShapeDtypeStruct
    return pl.pallas_call(
        hidden_back_kernel,
        out_shape=(
            shape((pages, rows, width), F32),
            shape((pages, 2 * HALF, width), BF16),
            shape((8, 3 * width), F32),
        ),
        grid=(pages,),
        in_specs=[
            page_block(rows + 2 * HALF, 3 * width),
            page_block(rows, width),
            whole(width, 3 * width),
        ],
        out_specs=[page_block(rows, width), page_block(2 * HALF, width), whole(8, 3 * width)],
        compiler_params=pltpu.CompilerParams(vmem_limit_bytes=40 << 20),
        cost_estimate=pl.CostEstimate(
            flops=2 * pages * rows * width * 3 * width, bytes_accessed=15 << 20, transcendentals=0
        ),
        name="hidden_backward",
    )(grad_mixed, grad_total, qkv_w)


def edge_kernel(band_ref, grad_ref, far_ref, got_ref, out_ref):
    side = pl.program_id(1)
    band = band_ref[0]
    far = far_ref[0].astype(F32)
    got = got_ref[0].astype(F32)
    low = jnp.where(band == 0, far[:HALF] + got[:HALF], got[HALF:])
    high = jnp.where(band == 0, got[HALF:], 0.0)
    add = jnp.where(side < 2, low, high)
    half = HALF // 2
    out_ref[0] = grad_ref[0] + jnp.where(side % 2 == 0, add[:half], add[half:])


def edge_add(band, grad, far, got):
    pages, rows, width = grad.shape
    half = HALF // 2
    last = rows // half - 2

    def edge(p, s, *_):
        return (p, jnp.where(s < 2, s, last + s - 2), 0)

    return pl.pallas_call(
        edge_kernel,
        out_shape=jax.ShapeDtypeStruct(grad.shape, F32),
        grid_spec=pltpu.PrefetchScalarGridSpec(
            num_scalar_prefetch=1,
            grid=(pages, 4),
            in_specs=[
                pl.BlockSpec((1, half, width), edge),
                page_block(2 * HALF, width),
                page_block(2 * HALF, width),
            ],
            out_specs=pl.BlockSpec((1, half, width), edge),
        ),
        input_output_aliases={1: 0},
        name="edge_add",
    )(band, grad, far, got)


def split_orders(count):
    total = count.bit_length() - 1
    side = total // 3
    x, y, z = (range(side), range(side, 2 * side), range(2 * side, total))
    near, far = list(z)[:-1], list(z)[-1:]
    return list(x) + list(y) + near + far, list(y) + near + list(x) + far


def place(chunk, order):
    spot = 0
    for level, bit in enumerate(order):
        spot = spot + (((chunk >> bit) & 1) << (len(order) - 1 - level))
    return spot


def product_parts(band, left, right, chunks):
    tokens, height = left.shape
    width = right.shape[1]
    size = height // chunks
    step = 384
    each = step // size
    half = chunks // 2
    orders = split_orders(half)

    def kernel(band_ref, l_ref, r_ref, send_ref, keep_ref):
        i = pl.program_id(0)
        result = dot(l_ref[...], r_ref[...], TN).astype(BF16)
        owner = (i >= pl.num_programs(0) // 2).astype(I32)

        def write(ref):
            for c in range(each):
                chunk = i * each + c - owner * half
                spot = jnp.where(owner == 0, place(chunk, orders[0]), place(chunk, orders[1]))
                ref[spot] = result[size * c : size * c + size]

        pl.when(owner == band_ref[0])(lambda: write(keep_ref))
        pl.when(owner != band_ref[0])(lambda: write(send_ref))

    out = jax.ShapeDtypeStruct((half, size, width), BF16)
    return pl.pallas_call(
        kernel,
        out_shape=(out, out),
        grid_spec=pltpu.PrefetchScalarGridSpec(
            num_scalar_prefetch=1,
            grid=(height // step,),
            in_specs=[pl.BlockSpec((tokens, step), lambda i, *_: (0, i)), whole(tokens, width)],
            out_specs=[whole(half, size, width), whole(half, size, width)],
        ),
        compiler_params=pltpu.CompilerParams(vmem_limit_bytes=40 << 20),
        cost_estimate=pl.CostEstimate(
            flops=2 * tokens * height * width, bytes_accessed=16 << 20, transcendentals=0
        ),
        name="product_parts",
    )(band, left, right)


def product_halves(band, left, right):
    tokens, height = left.shape
    width = right.shape[1]
    step = height // 2

    def kernel(band_ref, l_ref, r_ref, send_ref, keep_ref):
        result = dot(l_ref[...], r_ref[...], TN).astype(BF16)

        @pl.when(pl.program_id(0) == 0)
        def _():
            send_ref[...] = result

        @pl.when(pl.program_id(0) == 1)
        def _():
            keep_ref[...] = result

    out = jax.ShapeDtypeStruct((step, width), BF16)
    return pl.pallas_call(
        kernel,
        out_shape=(out, out),
        grid_spec=pltpu.PrefetchScalarGridSpec(
            num_scalar_prefetch=1,
            grid=(2,),
            in_specs=[
                pl.BlockSpec(
                    (tokens, step), lambda i, b: (0, jnp.where(i == 0, 1 - b[0], b[0]))
                ),
                whole(tokens, width),
            ],
            out_specs=[whole(step, width), whole(step, width)],
        ),
        compiler_params=pltpu.CompilerParams(vmem_limit_bytes=40 << 20),
        cost_estimate=pl.CostEstimate(
            flops=2 * tokens * height * width, bytes_accessed=16 << 20, transcendentals=0
        ),
        name="product_halves",
    )(band, left, right)


def swap_bands(block):
    return lax.ppermute(block, "band", [(0, 1), (1, 0)])


def swap_pages(block, level, orders):
    count = lax.axis_size("page")
    route = [
        (b * count + p, b * count + (p ^ (1 << orders[b][level])))
        for b in range(2)
        for p in range(count)
    ]
    return lax.ppermute(block, ("band", "page"), route)


def sides(orders):
    band, page = lax.axis_index("band"), lax.axis_index("page")
    return [
        jnp.where(band == 0, (page >> first) & 1, (page >> second) & 1)
        for first, second in zip(*orders)
    ]


def half_of(block, side):
    size = block.shape[0] // 2
    return lax.dynamic_slice_in_dim(block, side * size, size, 0)


def add_low(a, b):
    return (a.astype(F32) + b.astype(F32)).astype(BF16)


def scatter_sum(send, keep):
    orders = split_orders(lax.axis_size("page"))
    got = swap_bands(send)
    for level, side in enumerate(sides(orders)):
        sent = add_low(half_of(keep, 1 - side), half_of(got, 1 - side))
        keep = add_low(half_of(keep, side), half_of(got, side))
        got = swap_pages(sent, level, orders)
    return (keep.astype(F32) + got.astype(F32))[0]


def join(mine, other, side):
    return jnp.where(
        side == 0,
        jnp.concatenate([mine, other], axis=0),
        jnp.concatenate([other, mine], axis=0),
    )


def all_sum(send, keep):
    orders = split_orders(lax.axis_size("page"))
    got = swap_bands(send)
    places = sides(orders)
    for level, side in enumerate(places[:-1]):
        sent = add_low(half_of(keep, 1 - side), half_of(got, 1 - side))
        keep = add_low(half_of(keep, side), half_of(got, side))
        got = swap_pages(sent, level, orders)
    keep = add_low(keep, got)
    keep = add_low(keep, swap_pages(keep, len(places) - 1, orders))
    for level in reversed(range(len(places) - 1)):
        keep = join(keep, swap_pages(keep, level, orders), places[level])
    return join(keep, swap_bands(keep), lax.axis_index("band")).astype(F32)


def all_sum_small(block):
    orders = split_orders(lax.axis_size("page"))
    block = block + swap_bands(block)
    for level in range(len(orders[0])):
        block = block + swap_pages(block, level, orders)
    return block


def flat(block):
    return block.reshape(-1, block.shape[-1])


def local(
    hidden, cotangent, page_lengths, x_coord, line_ids, qkv_w, q_bias, v_bias,
    rel_table, x_table, y_table, out_w, out_b, ln1_gain, ln1_bias,
    ffn_in_w, ffn_in_b, ffn_out_w, ffn_out_b, ln2_gain, ln2_bias,
):
    pages, rows, width = hidden.shape
    band = lax.axis_index("band")
    chunks = 2 * lax.axis_size("page")
    band_arr = band.reshape(1).astype(I32)
    own_edge = jnp.where(band == 0, hidden[:, rows - HALF :], hidden[:, :HALF])
    got = swap_bands(jnp.concatenate([hidden[:, :HALF], own_edge], axis=1))
    context, probs, queries, pairs, extended = attention_forward(
        band_arr, page_lengths, hidden, got, x_coord, line_ids, qkv_w, q_bias, v_bias,
        (rel_table, x_table, y_table),
    )
    output, first, normed, inverse, act, slope, grad_total2, second_low, sums2 = ffn_forward(
        context, hidden, cotangent, (out_b, ln1_gain, ln1_bias, ffn_out_b, ln2_gain, ln2_bias),
        ffn_in_b, out_w, ffn_in_w, ffn_out_w,
    )
    grad_ffn_out = scatter_sum(*product_parts(band_arr, flat(act), flat(second_low), chunks))
    grad_inner, grad_total1, attn_low, grad_context, sums1, inner_sums = ffn_backward(
        second_low, slope, grad_total2, normed, inverse, ln1_gain, out_w, ffn_in_w, ffn_out_w
    )
    grad_ffn_in = scatter_sum(*product_parts(band_arr, flat(grad_inner), flat(first), chunks))
    grad_out = all_sum(*product_halves(band_arr, flat(context), flat(attn_low)))
    grad_mixed, grad_scores = attention_backward(probs, queries, pairs, grad_context)
    grad_qkv = all_sum(*product_halves(band_arr, flat(extended), flat(grad_mixed)))
    grad_hidden, far, mixed_sums = hidden_backward(grad_mixed, grad_total1, qkv_w)
    grad_hidden = edge_add(band_arr, grad_hidden, far, swap_bands(far))
    tables = table_sums(band_arr, grad_scores, x_coord, line_ids)
    small = jnp.concatenate(
        [
            mixed_sums[0].reshape(3, width),
            sums1[:3],
            sums2[:3],
            inner_sums[0].reshape(FF // width, width),
            jnp.pad(tables, ((0, 3), (0, width - tables.shape[1]))),
        ],
        axis=0,
    )
    small = all_sum_small(small)
    tables = small[13 : 13 + HEADS]
    return (
        output,
        grad_hidden,
        grad_qkv,
        small[0],
        small[2],
        tables[:, 128:160].T,
        tables[:, :64].T,
        tables[:, 64:128].T,
        grad_out,
        small[5],
        small[3],
        small[4],
        grad_ffn_in.T,
        small[9:13].reshape(FF),
        grad_ffn_out,
        small[8],
        small[6],
        small[7],
    )


def solution(mesh):
    in_specs = (
        P("page", "band", None),
        P("page", "band", None),
        P("page"),
        P("page", None),
        P("page", None),
        P(),
        P(),
        P(),
        P(),
        P(),
        P(),
        P(),
        P(),
        P(),
        P(),
        P(),
        P(),
        P(),
        P(),
        P(),
        P(),
    )
    out_specs = (
        P("page", "band", None),
        P("page", "band", None),
        P(),
        P(),
        P(),
        P(),
        P(),
        P(),
        P(),
        P(),
        P(),
        P(),
        P(None, ("band", "page")),
        P(),
        P(("band", "page"), None),
        P(),
        P(),
        P(),
    )
    return jax.shard_map(local, mesh=mesh, in_specs=in_specs, out_specs=out_specs, check_vma=False)
```

time: 876 us -> 340 us (0.39)
  matrix products: 336 us -> 0 us
  Pallas kernels: 0 us -> 189 us
  waiting for transfers between devices: 229 us -> 51 us
  local copies, waits for them, and re-layouts: 134 us -> 20.9 us
  other arithmetic: 99.3 us -> 38.4 us
  blocking collectives: 45.7 us -> 0 us
  starting transfers between devices: 12.3 us -> 38.5 us
  between operations: 14.8 us -> 1.19 us
    dot_general x24 -> x0, matrix products: 336 us -> none  [the longest x3 72.5 us: table_grads(): jnp.einsum('phqk,pqkc->ch', grad_scores_low, one_hots(bucket_ids, table.s...]
    unnamed x4 -> x0, waiting for transfers between devices: 204 us -> none
    pallas_call x0 -> x11, Pallas kernels: none -> 189 us  [the longest x1 40.8 us: table_sums(): pl.pallas_call(table_kernel, out_shape=jax.ShapeDtypeStruct((HEADS, bucke...]
    ppermute x5 -> x35, waiting for transfers between devices: 0.01 us -> 51 us  [the longest x26 47.2 us: swap_pages(): return lax.ppermute(block, ('band', 'page'), route)]
    psum x1 -> x0, blocking collectives: 45.7 us -> none  [local(): lax.psum((grad_qkv_w, grad_q_bias, grad_v_bias, grad_rel_table, grad_x_ta...]
    reshape x8 -> x10, local copies, waits for them, and re-layouts: 42.2 us -> 5.87 us  [the longest x6 3.49 us: ffn_forward(): v.reshape(1, width)]
    unnamed x115 -> x81, local copies, waits for them, and re-layouts: 44.2 us -> 11.8 us
    ppermute x5 -> x35, starting transfers between devices: 11.8 us -> 38.5 us  [the longest x26 31.9 us: swap_pages(): return lax.ppermute(block, ('band', 'page'), route)]
  transfers between devices with their start and end apart: 8 -> 35, of which waited for: 2 -> 13; matrix products, arithmetic and copies ran while one was open for 31% -> 12% of each run, Pallas kernels for 0% -> 23%
where the time goes in v1:
time: 340 us; the launch traced here: 339 us
  Pallas kernels  189 us (56%)
  waiting for transfers between devices  51 us (15%)
  starting transfers between devices  38.5 us (11%)
  other arithmetic  38.4 us (11%)
  local copies, waits for them, and re-layouts  20.9 us (6%)
    ppermute x26, waiting for transfers between devices, swap_pages(): return lax.ppermute(block, ('band', 'page'), route)  47.2 us
    pallas_call x1, Pallas kernels, table_sums(): pl.pallas_call(table_kernel, out_shape=jax.ShapeDtypeStruct((HEADS, bucke...  40.8 us
    pallas_call x1, Pallas kernels, attention_forward(): pl.pallas_call(attention_kernel, out_shape=(shape((pages, rows, width), B...  38.6 us
    ppermute x26, starting transfers between devices, swap_pages(): return lax.ppermute(block, ('band', 'page'), route)  31.9 us
    pallas_call x1, Pallas kernels, ffn_forward(): pl.pallas_call(ffn_forward_kernel, out_shape=(shape((pages, rows, width),...  27.1 us
    pallas_call x1, Pallas kernels, ffn_backward(): pl.pallas_call(ffn_backward_kernel, out_shape=(shape((pages, rows, FF), B...  24.3 us
    convert_element_type x18, other arithmetic, add_low(): return (a.astype(F32) + b.astype(F32)).astype(BF16)  22.3 us
    pallas_call x2, Pallas kernels, product_parts(): pl.pallas_call(kernel, out_shape=(out, out), grid_spec=pltpu.PrefetchScal...  18.5 us
  transfers between devices with their start and end apart: 35, of which 13 were waited for; matrix products, arithmetic and copies ran while one was open for 12% of the time, Pallas kernels for 23%

profile of v1, /device:TPU:0, one launch (start us, length us, event | category | flops | bytes accessed | tf_op | source)
XLA Modules:
  0.0 339.2 jit_solution(4022536745171519287)
XLA Ops:
  0.8 1.2 fusion.2
  10.7 38.6 %attention_forward.1 = (bf16[3,288,768]{2,1,0:T(8,128)(2,1)}, bf16[3,5,768,256]{3,2,1,0:T(8,128)(2,1)}, bf16[3,320,768]{2,1,0:T(8,128)(2,1)}, bf16[3,512,1536]{2,1,0:T(8,128)(2,1)}, bf16[3,416,768]{2,1,0:T(8,128)(2,1)}) custom-call(s32[1]{0:T(128)} %bitcast.band_ref, s32[3]{0:T(128)} %len_ref.1, bf16[3,288,768]{2,1,0:T(8,128)(2,1)} %hid_ref.3, ...), custom_call_target="tpu_custom_call" | custom-call | flops 7436500992 | bytes 31457280 | tf_op jit(solution)/shard_map/attention_forward/pallas_call | solution.py:279
  49.3 27.1 %ffn_forward.1 = (bf16[3,288,768]{2,1,0:T(8,128)(2,1)}, bf16[3,288,768]{2,1,0:T(8,128)(2,1)}, f32[3,288,768]{2,1,0:T(8,128)}, f32[3,288,128]{2,1,0:T(8,128)}, bf...) custom-call(bf16[3,288,768]{2,1,0:T(8,128)(2,1)} %get-tuple-element., ...), custom_call_target="tpu_custom_call" | custom-call | flops 9172942848 | bytes 41943040 | tf_op jit(solution)/shard_map/ffn_forward/pallas_call | solution.py:423
  76.4 24.3 %ffn_backward.1 = (bf16[3,288,3072]{2,1,0:T(8,128)(2,1)}, f32[3,288,768]{2,1,0:T(8,128)}, bf16[3,288,768]{2,1,0:T(8,128)(2,1)}, bf16[3,288,768]{2,1,0:T(8,128)(2...) custom-call(bf16[3,288,768]{2,1,0:T(8,128)(2,1)} %get-tuple-element.56.ds_ref, ...), custom_call_target="tpu_custom_call" | custom-call | flops 9172942848 | bytes 41943040 | tf_op jit(solution)/shard_map/ffn_backward/pallas_call | solution.py:509
  100.7 16.7 %attention_backward.1 = (bf16[3,416,2304]{2,1,0:T(8,128)(2,1)}, bf16[3,5,768,256]{3,2,1,0:T(8,128)(2,1)}) custom-call(bf16[3,5,768,256]{3,2,1,0:T(8,128)(2,1)} %get-tuple-element.53.p_ref, bf16[3,320,768]{2,1,0:T(8,128)(2,1)} %get-tuple-element.54.q_ref, bf16[3,512,1536]{2,1,0:T(8,128)(2,1)} %get-tuple-element.55.kv_ref, ...), custom_call_target="tpu_custom_call" | custom-call | flops 3774873600 | bytes 31457280 | tf_op jit(solution)/shard_map/attention_backward/pallas_call | solution.py:612
  117.4 2.6 copy-done
  120.0 5.6 %product_halves.2 = (bf16[384,2304]{1,0:T(8,128)(2,1)S(1)}, bf16[384,2304]{1,0:T(8,128)(2,1)S(1)}) custom-call(s32[1]{0:T(128)} %bitcast.band_ref, bf16[1248,768]{1,0:T(8,128)(2,1)S(1)} %bitcast.28, bf16[1248,2304]{1,0:T(8,128)(2,1)S(1)} %bitcast.21), custom_call_target="tpu_custom_call" | custom-call | flops 4416602112 | bytes 16777216 | tf_op jit(solution)/shard_map/product_halves/pallas_call | solution.py:869
  125.7 3.8 %collective-permute-done.2 = bf16[384,2304]{1,0:T(8,128)(2,1)} collective-permute-done((bf16[384,2304]{1,0:T(8,128)(2,1)S(1)}, bf16[384,2304]{1,0:T(8,128)(2,1)}, u32[]{:S(2)}, u32[]{:S(2)}) %collective-permute-start.2) | collective-permute-done | bytes 1769504 | tf_op jit(solution)/shard_map/ppermute | solution.py:892
  129.5 2.9 add_convert_fusion.5
  132.4 2.6 collective-permute-start.3
  135.0 2.5 copy-done.11
  137.5 9.3 %product_parts.3 = (bf16[16,96,768]{2,1,0:T(8,128)(2,1)}, bf16[16,96,768]{2,1,0:T(8,128)(2,1)S(1)}) custom-call(s32[1]{0:T(128)} %bitcast.band_ref, bf16[864,3072]{1,0:T(8,128)(2,1)S(1)} %bitcast.27, bf16[864,768]{1,0:T(8,128)(2,1)S(1)} %bitcast.31), custom_call_target="tpu_custom_call" | custom-call | flops 4076863488 | bytes 16777216 | tf_op jit(solution)/shard_map/product_parts/pallas_call | solution.py:835
  146.9 2.0 product_halves.3
  149.3 2.8 copy-done.17
  152.2 40.8 %table_sums.1 = f32[12,160]{1,0:T(8,128)S(1)} custom-call(s32[1]{0:T(128)} %bitcast.band_ref, bf16[3,5,768,256]{3,2,1,0:T(8,128)(2,1)S(1)} %copy-done.17, s32[3,576]{1,0:T(4,128)S(1)} %copy-done.9, s32[3,576]{1,0:T(4,128)S(1)} %copy-done.10), custom_call_target="tpu_custom_call" | custom-call | flops 5662310400 | bytes 6291456 | tf_op jit(solution)/shard_map/table_sums/pallas_call | solution.py:699
  193.0 1.0 add_convert_fusion.11
  194.1 1.5 collective-permute-start.4
  195.6 9.3 %product_parts.2 = (bf16[16,96,768]{2,1,0:T(8,128)(2,1)}, bf16[16,96,768]{2,1,0:T(8,128)(2,1)S(1)}) custom-call(s32[1]{0:T(128)} %bitcast.band_ref, bf16[864,3072]{1,0:T(8,128)(2,1)S(1)} %bitcast.26, bf16[864,768]{1,0:T(8,128)(2,1)S(1)} %bitcast.29), custom_call_target="tpu_custom_call" | custom-call | flops 4076863488 | bytes 16777216 | tf_op jit(solution)/shard_map/product_parts/pallas_call | solution.py:835
  204.9 7.9 %hidden_backward.1 = (f32[3,288,768]{2,1,0:T(8,128)}, bf16[3,128,768]{2,1,0:T(8,128)(2,1)S(1)}, f32[8,2304]{1,0:T(8,128)S(1)}) custom-call(bf16[3,416,2304]{2,1,0:T(8,128)(2,1)S(1)} %bitcast.23, f32[3,288,768]{2,1,0:T(8,128)S(1)} %copy-done.2, bf16[768,2304]{1,0:T(8,128)(2,1)S(1)} %copy-done.1), custom_call_target="tpu_custom_call" | custom-call | flops 3057647616 | bytes 15728640 | tf_op jit(solution)/shard_map/hidden_backward/pallas_call | solution.py:736
  213.7 1.0 add_convert_fusion.20
  214.7 1.6 collective-permute-start.5
  216.3 0.9 slice_reduce_fusion
  217.4 1.2 add_convert_fusion.17
  219.2 1.5 collective-permute-done.5
  220.7 1.0 add_convert_fusion.19
  221.7 2.6 collective-permute-start.6
  226.6 7.4 %collective-permute-done.6 = bf16[48,2304]{1,0:T(8,128)(2,1)} collective-permute-done((bf16[48,2304]{1,0:T(8,128)(2,1)S(1)}, bf16[48,2304]{1,0:T(8,128)(2,1)}, u32[]{:S(2)}, u32[]{:S(2)}) %collective-permute-start.6) | collective-permute-done | bytes 221216 | tf_op jit(solution)/shard_map/ppermute | solution.py:902
  234.0 1.0 add_convert_fusion.18
  235.1 1.5 collective-permute-start.12
  236.7 4.2 %collective-permute-done.12 = f32[28,768]{1,0:T(8,128)S(1)} collective-permute-done((f32[28,768]{1,0:T(8,128)S(1)}, f32[28,768]{1,0:T(8,128)S(1)}, u32[]{:S(2)}, u32[]{:S(2)}) %collective-permute-start.12) | collective-permute-done | bytes 86048 | tf_op jit(solution)/shard_map/ppermute | solution.py:902
  240.9 1.5 collective-permute-start.13
  242.4 1.0 collective-permute-start.19
  244.1 4.3 %collective-permute-done.19 = bf16[48,768]{1,0:T(8,128)(2,1)S(1)} collective-permute-done((bf16[48,768]{1,0:T(8,128)(2,1)S(1)}, bf16[48,768]{1,0:T(8,128)(2,1)S(1)}, u32[]{:S(2)}, u32[]{:S(2)}) %collective-permute-start.19) | collective-permute-done | bytes 73760 | tf_op jit(solution)/shard_map/ppermute | solution.py:902
  248.5 1.3 collective-permute-start.20
  249.8 3.5 %add_convert_fusion.1 = (bf16[8,96,768]{2,1,0:T(8,128)(2,1)S(1)}, bf16[8,96,768]{2,1,0:T(8,128)(2,1)}) fusion(bf16[16,96,768]{2,1,0:T(8,128)(2,1)} %collective-permute-done.30, s32[]{:T(128)S(6)} %select_n.204, bf16[16,96,768]{2,1,0:T(8,128)(2,1)S(1)} %copy-done.4, s32[]{:T(128)S(6)} %select_n.206), kind=kLoop, calls=%fused_computation.3 | loop fusion | flops 4718592 | bytes 7077896 | tf_op jit(solution)/shard_map/convert_element_type | solution.py:919
  253.9 3.3 add_convert_fusion.3
  257.2 1.5 collective-permute-start.26
  258.7 1.1 maximum_select_fusion.3
  260.3 1.3 collective-permute-start.21
  262.5 2.2 collective-permute-done.21
  264.8 1.6 collective-permute-start.22
  266.4 0.9 collective-permute-done.14
  267.2 1.6 collective-permute-start.15
  268.8 5.0 %collective-permute-done.15 = f32[28,768]{1,0:T(8,128)S(1)} collective-permute-done((f32[28,768]{1,0:T(8,128)S(1)}, f32[28,768]{1,0:T(8,128)S(1)}, u32[]{:S(2)}, u32[]{:S(2)}) %collective-permute-start.15) | collective-permute-done | bytes 86048 | tf_op jit(solution)/shard_map/ppermute | solution.py:902
  274.0 1.5 collective-permute-start.23
  275.5 1.5 add_convert_fusion.7
  277.7 6.6 %collective-permute-done.26 = bf16[8,96,768]{2,1,0:T(8,128)(2,1)} collective-permute-done((bf16[8,96,768]{2,1,0:T(8,128)(2,1)}, bf16[8,96,768]{2,1,0:T(8,128)(2,1)}, u32[]{:S(2)}, u32[]{:S(2)}) %collective-permute-start.26) | collective-permute-done | bytes 1179680 | tf_op jit(solution)/shard_map/ppermute | solution.py:902
  284.3 1.5 add_convert_fusion.9
  286.5 7.3 %collective-permute-done.9 = bf16[192,2304]{1,0:T(8,128)(2,1)} collective-permute-done((bf16[192,2304]{1,0:T(8,128)(2,1)}, bf16[192,2304]{1,0:T(8,128)(2,1)}, u32[]{:S(2)}, u32[]{:S(2)}) %collective-permute-start.9) | collective-permute-done | bytes 884768 | tf_op jit(solution)/shard_map/ppermute | solution.py:902
  293.8 2.4 maximum_select_fusion.1
  296.2 2.0 collective-permute-start.10
  299.1 3.2 collective-permute-start.24
  303.2 2.5 collective-permute-start.33
  306.3 0.8 add_convert_fusion.15
  308.4 7.8 %edge_add.1 = f32[3,288,768]{2,1,0:T(8,128)} custom-call(s32[1]{0:T(128)} %bitcast.band_ref, f32[3,288,768]{2,1,0:T(8,128)} %get-tuple-element.64.grad_ref, bf16[3,128,768]{2,1,0:T(8,128)(2,1)} %copy-done.7, bf16[3,128,768]{2,1,0:T(8,128)(2,1)} %collective-permute-done.1.got_ref), custom_call_target="tpu_custom_call", output_to_operand_aliasing={{}: (1, {})} | custom-call | tf_op jit(solution)/shard_map/edge_add/pallas_call | solution.py:778
  316.2 0.9 add_convert_fusion.22
  317.2 2.6 collective-permute-start.34
  319.8 2.9 fusion.1
  322.7 0.9 add_convert_fusion.24
  324.0 2.4 collective-permute-done.34
  326.5 1.7 add_bitcast_fusion
  328.1 4.6 %collective-permute-done.29 = bf16[1,96,768]{2,1,0:T(8,128)(2,1)S(1)} collective-permute-done((bf16[1,96,768]{2,1,0:T(8,128)(2,1)S(1)}, bf16[1,96,768]{2,1,0:T(8,128)(2,1)S(1)}, u32[]{:S(2)}, u32[]{:S(2)}) %collective-permute-start.29) | collective-permute-done | bytes 147488 | tf_op jit(solution)/shard_map/ppermute | solution.py:902
  332.8 1.7 add_bitcast_fusion.1
  334.4 4.8 %fusion = f32[768,2304]{1,0:T(8,128)} fusion(bf16[384,2304]{1,0:T(8,128)(2,1)} %collective-permute-done.10, bf16[384,2304]{1,0:T(8,128)(2,1)S(1)} %maximum_select_fusion.1, pred[]{:T(512)S(6)} %eq.8), kind=kLoop, calls=%fused_computation.1 | loop fusion | flops 17694720 | bytes 10616833 | tf_op jit(solution)/shard_map/convert_element_type | solution.py:952
  (157 shorter events, 21.6 us)
Async XLA Ops:
  0.7 3.0 copy-start.28
  0.7 3.6 %copy-start.29 = (bf16[768]{0:T(1024)(128)(2,1)S(1)}, bf16[768]{0:T(1024)(128)(2,1)}, u32[]{:S(2)}) copy-start(bf16[768]{0:T(1024)(128)(2,1)} %param.33) | copy-start | bytes 4612
  0.7 4.2 %copy-start.30 = (bf16[768]{0:T(1024)(128)(2,1)S(1)}, bf16[768]{0:T(1024)(128)(2,1)}, u32[]{:S(2)}) copy-start(bf16[768]{0:T(1024)(128)(2,1)} %param.35) | copy-start | bytes 4612
  0.7 4.7 %copy-start.31 = (bf16[768]{0:T(1024)(128)(2,1)S(1)}, bf16[768]{0:T(1024)(128)(2,1)}, u32[]{:S(2)}) copy-start(bf16[768]{0:T(1024)(128)(2,1)} %param.39) | copy-start | bytes 4612
  0.7 5.3 %copy-start.32 = (bf16[768]{0:T(1024)(128)(2,1)S(1)}, bf16[768]{0:T(1024)(128)(2,1)}, u32[]{:S(2)}) copy-start(bf16[768]{0:T(1024)(128)(2,1)} %param.40) | copy-start | bytes 4612
  0.7 5.9 %copy-start.33 = (bf16[768]{0:T(1024)(128)(2,1)S(1)}, bf16[768]{0:T(1024)(128)(2,1)}, u32[]{:S(2)}) copy-start(bf16[768]{0:T(1024)(128)(2,1)} %param.41) | copy-start | bytes 4612
  0.7 6.5 %copy-start.23 = (bf16[32,12]{0,1:T(8,128)(2,1)S(1)}, bf16[32,12]{0,1:T(8,128)(2,1)}, u32[]{:S(2)}) copy-start(bf16[32,12]{0,1:T(8,128)(2,1)} %param.29) | copy-start | bytes 2308
  0.8 7.1 %copy-start.22 = (bf16[3072]{0:T(1024)(128)(2,1)S(1)}, bf16[3072]{0:T(1024)(128)(2,1)}, u32[]{:S(2)}) copy-start(bf16[3072]{0:T(1024)(128)(2,1)} %param.37) | copy-start | bytes 18436
  0.8 7.7 %copy-start.24 = (bf16[64,12]{0,1:T(8,128)(2,1)S(1)}, bf16[64,12]{0,1:T(8,128)(2,1)}, u32[]{:S(2)}) copy-start(bf16[64,12]{0,1:T(8,128)(2,1)} %param.30) | copy-start | bytes 4612
  0.8 8.4 %copy-start.25 = (bf16[64,12]{0,1:T(8,128)(2,1)S(1)}, bf16[64,12]{0,1:T(8,128)(2,1)}, u32[]{:S(2)}) copy-start(bf16[64,12]{0,1:T(8,128)(2,1)} %param.31) | copy-start | bytes 4612
  2.0 7.9 %collective-permute-start = (bf16[3,128,768]{2,1,0:T(8,128)(2,1)S(1)}, bf16[3,128,768]{2,1,0:T(8,128)(2,1)S(1)}, u32[]{:S(2)}, u32[]{:S(2)}) collective-permute-start(bf16[3,128,768]{2,1,0:T(8,128)(2,1)S(1)} %pad_maximum_fusion), channel_id=1, source_target_pairs={{0,16},{16,0},{1,17},{17,1},{2,18},{18,2},{3,19},{19,3},{4,20},{20... | collective-permute-start | bytes 1769480 | tf_op jit(solution)/shard_map/ppermute | solution.py:892
  100.7 16.7 %copy-start.12 = (bf16[3,416,768]{2,1,0:T(8,128)(2,1)S(1)}, bf16[3,416,768]{2,1,0:T(8,128)(2,1)}, u32[]{:S(2)}) copy-start(bf16[3,416,768]{2,1,0:T(8,128)(2,1)} %get-tuple-element.66) | copy-start | bytes 5750788
  125.6 3.9 %collective-permute-start.2 = (bf16[384,2304]{1,0:T(8,128)(2,1)S(1)}, bf16[384,2304]{1,0:T(8,128)(2,1)}, u32[]{:S(2)}, u32[]{:S(2)}) collective-permute-start(bf16[384,2304]{1,0:T(8,128)(2,1)S(1)} %get-tuple-element.68), channel_id=1, source_target_pairs={{0,16},{16,0},{1,17},{17,1},{2,18},{18,2},{3,19},{19,3},{4,20},{20... | collective-permute-start | bytes 5308424 | tf_op jit(solution)/shard_map/ppermute | solution.py:892
  129.5 5.5 %copy-start.15 = (bf16[3,288,768]{2,1,0:T(8,128)(2,1)S(1)}, bf16[3,288,768]{2,1,0:T(8,128)(2,1)}, u32[]{:S(2)}) copy-start(bf16[3,288,768]{2,1,0:T(8,128)(2,1)} %get-tuple-element.56.ds_ref) | copy-start | bytes 3981316
  132.4 60.7 %collective-permute-start.3 = (bf16[192,2304]{1,0:T(8,128)(2,1)}, bf16[192,2304]{1,0:T(8,128)(2,1)S(1)}, u32[]{:S(2)}, u32[]{:S(2)}) collective-permute-start(bf16[192,2304]{1,0:T(8,128)(2,1)} %get-tuple-element.97), channel_id=1, source_target_pairs={{0,1},{1,0},{2,3},{3,2},{4,5},{5,4},{6,7},{7,6},{8,9},{9,8},{10,11... | collective-permute-start | bytes 2654216 | tf_op jit(solution)/shard_map/ppermute | solution.py:902
  137.5 9.4 %copy-start.14 = (bf16[3,288,768]{2,1,0:T(8,128)(2,1)S(1)}, bf16[3,288,768]{2,1,0:T(8,128)(2,1)}, u32[]{:S(2)}) copy-start(bf16[3,288,768]{2,1,0:T(8,128)(2,1)} %get-tuple-element.51.ctx_ref) | copy-start | bytes 3981316
  137.5 9.4 %copy-start.16 = (bf16[3,288,768]{2,1,0:T(8,128)(2,1)S(1)}, bf16[3,288,768]{2,1,0:T(8,128)(2,1)}, u32[]{:S(2)}) copy-start(bf16[3,288,768]{2,1,0:T(8,128)(2,1)} %get-tuple-element.74) | copy-start | bytes 3981316
  146.8 103.1 %collective-permute-start.30 = (bf16[16,96,768]{2,1,0:T(8,128)(2,1)}, bf16[16,96,768]{2,1,0:T(8,128)(2,1)}, u32[]{:S(2)}, u32[]{:S(2)}) collective-permute-start(bf16[16,96,768]{2,1,0:T(8,128)(2,1)} %get-tuple-element.83), channel_id=1, source_target_pairs={{0,16},{16,0},{1,17},{17,1},{2,18},{18,2},{3,19},{19,3},{4,20},{20... | collective-permute-start | bytes 7077896 | tf_op jit(solution)/shard_map/ppermute | solution.py:892
  148.9 68.5 %collective-permute-start.16 = (bf16[384,768]{1,0:T(8,128)(2,1)S(1)}, bf16[384,768]{1,0:T(8,128)(2,1)}, u32[]{:S(2)}, u32[]{:S(2)}) collective-permute-start(bf16[384,768]{1,0:T(8,128)(2,1)S(1)} %get-tuple-element.76), channel_id=1, source_target_pairs={{0,16},{16,0},{1,17},{17,1},{2,18},{18,2},{3,19},{19,3},{4,20},{20... | collective-permute-start | bytes 1769480 | tf_op jit(solution)/shard_map/ppermute | solution.py:892
  149.3 46.3 %slice-start.2 = ((s8[5308416]{0:T(1024)(128)(4,1)}), s8[4194304]{0:T(1024)(128)(4,1)S(1)}, s32[]{:S(2)}) async-start(s8[5308416]{0:T(1024)(128)(4,1)} %bitcast.24), calls=%async_computation.2 | async-start | bytes 8388608
  149.3 2.8 copy-start.17
  152.2 43.4 %slice-start.3 = ((s8[5308416]{0:T(1024)(128)(4,1)}), s8[1114112]{0:T(1024)(128)(4,1)S(1)}, s32[]{:S(2)}) async-start(s8[5308416]{0:T(1024)(128)(4,1)} %bitcast.24), calls=%async_computation.3 | async-start | bytes 2228224
  193.0 11.9 %slice-start = ((s8[5750784]{0:T(1024)(128)(4,1)}), s8[4194304]{0:T(1024)(128)(4,1)S(1)}, s32[]{:S(2)}) async-start(s8[5750784]{0:T(1024)(128)(4,1)} %bitcast.22), calls=%async_computation | async-start | bytes 8388608
  194.1 19.6 %copy-start.18 = (bf16[96,2304]{1,0:T(8,128)(2,1)}, bf16[96,2304]{1,0:T(8,128)(2,1)S(1)}, u32[]{:S(2)}) copy-start(bf16[96,2304]{1,0:T(8,128)(2,1)S(1)} %get-tuple-element.102) | copy-start | bytes 1327108
  194.1 19.6 %collective-permute-start.4 = (bf16[96,2304]{1,0:T(8,128)(2,1)}, bf16[96,2304]{1,0:T(8,128)(2,1)}, u32[]{:S(2)}, u32[]{:S(2)}) collective-permute-start(bf16[96,2304]{1,0:T(8,128)(2,1)} %get-tuple-element.103), channel_id=1, source_target_pairs={{0,2},{1,3},{2,0},{3,1},{4,6},{5,7},{6,4},{7,5},{8,10},{9,11},{10,... | collective-permute-start | bytes 1327112 | tf_op jit(solution)/shard_map/ppermute | solution.py:902
  195.6 9.3 %slice-start.1 = ((s8[5750784]{0:T(1024)(128)(4,1)}), s8[1556480]{0:T(1024)(128)(4,1)S(1)}, s32[]{:S(2)}) async-start(s8[5750784]{0:T(1024)(128)(4,1)} %bitcast.22), calls=%async_computation.1 | async-start | bytes 3112960
  195.6 9.3 %copy-start.1 = (bf16[768,2304]{1,0:T(8,128)(2,1)S(1)}, bf16[768,2304]{1,0:T(8,128)(2,1)}, u32[]{:S(2)}) copy-start(bf16[768,2304]{1,0:T(8,128)(2,1)} %w_ref.3) | copy-start | bytes 10616836
  195.6 9.3 %copy-start.2 = (f32[3,288,768]{2,1,0:T(8,128)S(1)}, f32[3,288,768]{2,1,0:T(8,128)}, u32[]{:S(2)}) copy-start(f32[3,288,768]{2,1,0:T(8,128)} %get-tuple-element.63.dh_ref) | copy-start | bytes 7962628
  204.9 7.9 %copy-start.5 = (bf16[16,96,768]{2,1,0:T(8,128)(2,1)}, bf16[16,96,768]{2,1,0:T(8,128)(2,1)S(1)}, u32[]{:S(2)}) copy-start(bf16[16,96,768]{2,1,0:T(8,128)(2,1)S(1)} %get-tuple-element.79) | copy-start | bytes 7077892
  204.9 8.7 %copy-start.20 = (f32[8,768]{1,0:T(8,128)S(1)}, f32[8,768]{1,0:T(8,128)}, u32[]{:S(2)}) copy-start(f32[8,768]{1,0:T(8,128)} %get-tuple-element.71) | copy-start | bytes 73732
  204.9 8.7 %copy-start.21 = (f32[8,768]{1,0:T(8,128)S(1)}, f32[8,768]{1,0:T(8,128)}, u32[]{:S(2)}) copy-start(f32[8,768]{1,0:T(8,128)} %get-tuple-element.70) | copy-start | bytes 73732
  214.7 6.0 %copy-start.19 = (bf16[96,2304]{1,0:T(8,128)(2,1)S(1)}, bf16[96,2304]{1,0:T(8,128)(2,1)}, u32[]{:S(2)}) copy-start(bf16[96,2304]{1,0:T(8,128)(2,1)} %copy-done.18) | copy-start | bytes 1327108
  214.7 6.0 %collective-permute-start.5 = (bf16[48,2304]{1,0:T(8,128)(2,1)S(1)}, bf16[48,2304]{1,0:T(8,128)(2,1)S(1)}, u32[]{:S(2)}, u32[]{:S(2)}) collective-permute-start(bf16[48,2304]{1,0:T(8,128)(2,1)S(1)} %add_convert_fusion.20), channel_id=1, source_target_pairs={{0,4},{1,5},{2,6},{3,7},{4,0},{5,1},{6,2},{7,3},{8,12},{9,13},{10,... | collective-permute-start | bytes 663560 | tf_op jit(solution)/shard_map/ppermute | solution.py:902
  217.3 36.6 %collective-permute-start.25 = (bf16[16,96,768]{2,1,0:T(8,128)(2,1)}, bf16[16,96,768]{2,1,0:T(8,128)(2,1)}, u32[]{:S(2)}, u32[]{:S(2)}) collective-permute-start(bf16[16,96,768]{2,1,0:T(8,128)(2,1)} %get-tuple-element.80), channel_id=1, source_target_pairs={{0,16},{16,0},{1,17},{17,1},{2,18},{18,2},{3,19},{19,3},{4,20},{20... | collective-permute-start | bytes 7077896 | tf_op jit(solution)/shard_map/ppermute | solution.py:892
  218.6 6.8 %collective-permute-start.17 = (bf16[192,768]{1,0:T(8,128)(2,1)S(1)}, bf16[192,768]{1,0:T(8,128)(2,1)S(1)}, u32[]{:S(2)}, u32[]{:S(2)}) collective-permute-start(bf16[192,768]{1,0:T(8,128)(2,1)S(1)} %get-tuple-element.111), channel_id=1, source_target_pairs={{0,1},{1,0},{2,3},{3,2},{4,5},{5,4},{6,7},{7,6},{8,9},{9,8},{10,11... | collective-permute-start | bytes 884744 | tf_op jit(solution)/shard_map/ppermute | solution.py:902
  221.7 12.3 %collective-permute-start.6 = (bf16[48,2304]{1,0:T(8,128)(2,1)S(1)}, bf16[48,2304]{1,0:T(8,128)(2,1)}, u32[]{:S(2)}, u32[]{:S(2)}) collective-permute-start(bf16[48,2304]{1,0:T(8,128)(2,1)S(1)} %add_convert_fusion.19), channel_id=1, source_target_pairs={{0,8},{1,9},{2,10},{3,11},{4,12},{5,13},{6,14},{7,15},{8,0},{9,1},... | collective-permute-start | bytes 663560 | tf_op jit(solution)/shard_map/ppermute | solution.py:902
  224.7 10.3 %collective-permute-start.11 = (f32[28,768]{1,0:T(8,128)S(1)}, f32[28,768]{1,0:T(8,128)S(1)}, u32[]{:S(2)}, u32[]{:S(2)}) collective-permute-start(f32[28,768]{1,0:T(8,128)S(1)} %concatenate.63), channel_id=1, source_target_pairs={{0,16},{16,0},{1,17},{17,1},{2,18},{18,2},{3,19},{19,3},{4,20},{20... | collective-permute-start | bytes 258056 | tf_op jit(solution)/shard_map/ppermute | solution.py:892
  225.3 24.5 %copy-start.4 = (bf16[16,96,768]{2,1,0:T(8,128)(2,1)S(1)}, bf16[16,96,768]{2,1,0:T(8,128)(2,1)}, u32[]{:S(2)}) copy-start(bf16[16,96,768]{2,1,0:T(8,128)(2,1)} %copy-done.3) | copy-start | bytes 7077892
  226.1 16.3 %collective-permute-start.18 = (bf16[96,768]{1,0:T(8,128)(2,1)}, bf16[96,768]{1,0:T(8,128)(2,1)S(1)}, u32[]{:S(2)}, u32[]{:S(2)}) collective-permute-start(bf16[96,768]{1,0:T(8,128)(2,1)} %get-tuple-element.113), channel_id=1, source_target_pairs={{0,2},{1,3},{2,0},{3,1},{4,6},{5,7},{6,4},{7,5},{8,10},{9,11},{10,... | collective-permute-start | bytes 442376 | tf_op jit(solution)/shard_map/ppermute | solution.py:902
  235.0 8.4 %collective-permute-start.7 = (bf16[48,2304]{1,0:T(8,128)(2,1)S(1)}, bf16[48,2304]{1,0:T(8,128)(2,1)S(1)}, u32[]{:S(2)}, u32[]{:S(2)}) collective-permute-start(bf16[48,2304]{1,0:T(8,128)(2,1)S(1)} %add_convert_fusion.18), channel_id=1, source_target_pairs={{0,4},{1,5},{2,6},{3,7},{4,0},{5,1},{6,2},{7,3},{8,12},{9,13},{10,... | collective-permute-start | bytes 663560 | tf_op jit(solution)/shard_map/ppermute | solution.py:902
  235.1 5.8 %collective-permute-start.12 = (f32[28,768]{1,0:T(8,128)S(1)}, f32[28,768]{1,0:T(8,128)S(1)}, u32[]{:S(2)}, u32[]{:S(2)}) collective-permute-start(f32[28,768]{1,0:T(8,128)S(1)} %add.218), channel_id=1, source_target_pairs={{0,1},{1,0},{2,3},{3,2},{4,5},{5,4},{6,7},{7,6},{8,9},{9,8},{10,11... | collective-permute-start | bytes 258056 | tf_op jit(solution)/shard_map/ppermute | solution.py:902
  240.9 20.7 %collective-permute-start.13 = (f32[28,768]{1,0:T(8,128)S(1)}, f32[28,768]{1,0:T(8,128)S(1)}, u32[]{:S(2)}, u32[]{:S(2)}) collective-permute-start(f32[28,768]{1,0:T(8,128)S(1)} %add.219), channel_id=1, source_target_pairs={{0,2},{1,3},{2,0},{3,1},{4,6},{5,7},{6,4},{7,5},{8,10},{9,11},{10,... | collective-permute-start | bytes 258056 | tf_op jit(solution)/shard_map/ppermute | solution.py:902
  242.4 6.1 %collective-permute-start.19 = (bf16[48,768]{1,0:T(8,128)(2,1)S(1)}, bf16[48,768]{1,0:T(8,128)(2,1)S(1)}, u32[]{:S(2)}, u32[]{:S(2)}) collective-permute-start(bf16[48,768]{1,0:T(8,128)(2,1)S(1)} %add_convert_fusion.30), channel_id=1, source_target_pairs={{0,4},{1,5},{2,6},{3,7},{4,0},{5,1},{6,2},{7,3},{8,12},{9,13},{10,... | collective-permute-start | bytes 221192 | tf_op jit(solution)/shard_map/ppermute | solution.py:902
  243.5 15.2 %collective-permute-start.8 = (bf16[96,2304]{1,0:T(8,128)(2,1)S(1)}, bf16[96,2304]{1,0:T(8,128)(2,1)S(1)}, u32[]{:S(2)}, u32[]{:S(2)}) collective-permute-start(bf16[96,2304]{1,0:T(8,128)(2,1)S(1)} %maximum_select_fusion.5), channel_id=1, source_target_pairs={{0,2},{1,3},{2,0},{3,1},{4,6},{5,7},{6,4},{7,5},{8,10},{9,11},{10,... | collective-permute-start | bytes 1327112 | tf_op jit(solution)/shard_map/ppermute | solution.py:902
  248.5 11.8 %collective-permute-start.20 = (bf16[48,768]{1,0:T(8,128)(2,1)S(1)}, bf16[48,768]{1,0:T(8,128)(2,1)S(1)}, u32[]{:S(2)}, u32[]{:S(2)}) collective-permute-start(bf16[48,768]{1,0:T(8,128)(2,1)S(1)} %add_convert_fusion.29), channel_id=1, source_target_pairs={{0,8},{1,9},{2,10},{3,11},{4,12},{5,13},{6,14},{7,15},{8,0},{9,1},... | collective-permute-start | bytes 221192 | tf_op jit(solution)/shard_map/ppermute | solution.py:902
  249.8 4.0 %copy-start.6 = (bf16[16,96,768]{2,1,0:T(8,128)(2,1)S(1)}, bf16[16,96,768]{2,1,0:T(8,128)(2,1)}, u32[]{:S(2)}) copy-start(bf16[16,96,768]{2,1,0:T(8,128)(2,1)} %copy-done.5) | copy-start | bytes 7077892
  253.3 22.2 %collective-permute-start.31 = (bf16[8,96,768]{2,1,0:T(8,128)(2,1)}, bf16[8,96,768]{2,1,0:T(8,128)(2,1)}, u32[]{:S(2)}, u32[]{:S(2)}) collective-permute-start(bf16[8,96,768]{2,1,0:T(8,128)(2,1)} %get-tuple-element.93), channel_id=1, source_target_pairs={{0,1},{1,0},{2,3},{3,2},{4,5},{5,4},{6,7},{7,6},{8,9},{9,8},{10,11... | collective-permute-start | bytes 3538952 | tf_op jit(solution)/shard_map/ppermute | solution.py:902
  257.2 16.7 %copy-start.8 = (bf16[3,128,768]{2,1,0:T(8,128)(2,1)S(1)}, bf16[3,128,768]{2,1,0:T(8,128)(2,1)}, u32[]{:S(2)}) copy-start(bf16[3,128,768]{2,1,0:T(8,128)(2,1)} %copy-done.7) | copy-start | bytes 1769476
  257.2 27.1 %collective-permute-start.26 = (bf16[8,96,768]{2,1,0:T(8,128)(2,1)}, bf16[8,96,768]{2,1,0:T(8,128)(2,1)}, u32[]{:S(2)}, u32[]{:S(2)}) collective-permute-start(bf16[8,96,768]{2,1,0:T(8,128)(2,1)} %get-tuple-element.95), channel_id=1, source_target_pairs={{0,1},{1,0},{2,3},{3,2},{4,5},{5,4},{6,7},{7,6},{8,9},{9,8},{10,11... | collective-permute-start | bytes 3538952 | tf_op jit(solution)/shard_map/ppermute | solution.py:902
  259.7 34.1 %collective-permute-start.9 = (bf16[192,2304]{1,0:T(8,128)(2,1)}, bf16[192,2304]{1,0:T(8,128)(2,1)}, u32[]{:S(2)}, u32[]{:S(2)}) collective-permute-start(bf16[192,2304]{1,0:T(8,128)(2,1)} %maximum_select_fusion.3), channel_id=1, source_target_pairs={{0,1},{1,0},{2,3},{3,2},{4,5},{5,4},{6,7},{7,6},{8,9},{9,8},{10,11... | collective-permute-start | bytes 2654216 | tf_op jit(solution)/shard_map/ppermute | solution.py:902
  260.3 4.4 %collective-permute-start.21 = (bf16[48,768]{1,0:T(8,128)(2,1)S(1)}, bf16[48,768]{1,0:T(8,128)(2,1)S(1)}, u32[]{:S(2)}, u32[]{:S(2)}) collective-permute-start(bf16[48,768]{1,0:T(8,128)(2,1)S(1)} %add_convert_fusion.28), channel_id=1, source_target_pairs={{0,4},{1,5},{2,6},{3,7},{4,0},{5,1},{6,2},{7,3},{8,12},{9,13},{10,... | collective-permute-start | bytes 221192 | tf_op jit(solution)/shard_map/ppermute | solution.py:902
  261.6 5.6 %collective-permute-start.14 = (f32[28,768]{1,0:T(8,128)S(1)}, f32[28,768]{1,0:T(8,128)S(1)}, u32[]{:S(2)}, u32[]{:S(2)}) collective-permute-start(f32[28,768]{1,0:T(8,128)S(1)} %add.220), channel_id=1, source_target_pairs={{0,4},{1,5},{2,6},{3,7},{4,0},{5,1},{6,2},{7,3},{8,12},{9,13},{10,... | collective-permute-start | bytes 258056 | tf_op jit(solution)/shard_map/ppermute | solution.py:902
  264.8 9.1 %collective-permute-start.22 = (bf16[96,768]{1,0:T(8,128)(2,1)S(1)}, bf16[96,768]{1,0:T(8,128)(2,1)S(1)}, u32[]{:S(2)}, u32[]{:S(2)}) collective-permute-start(bf16[96,768]{1,0:T(8,128)(2,1)S(1)} %maximum_select_fusion.7), channel_id=1, source_target_pairs={{0,2},{1,3},{2,0},{3,1},{4,6},{5,7},{6,4},{7,5},{8,10},{9,11},{10,... | collective-permute-start | bytes 442376 | tf_op jit(solution)/shard_map/ppermute | solution.py:902
  267.2 6.6 %collective-permute-start.15 = (f32[28,768]{1,0:T(8,128)S(1)}, f32[28,768]{1,0:T(8,128)S(1)}, u32[]{:S(2)}, u32[]{:S(2)}) collective-permute-start(f32[28,768]{1,0:T(8,128)S(1)} %add.221), channel_id=1, source_target_pairs={{0,8},{1,9},{2,10},{3,11},{4,12},{5,13},{6,14},{7,15},{8,0},{9,1},... | collective-permute-start | bytes 258056 | tf_op jit(solution)/shard_map/ppermute | solution.py:902
  273.9 34.5 %collective-permute-start.1 = (bf16[3,128,768]{2,1,0:T(8,128)(2,1)S(1)}, bf16[3,128,768]{2,1,0:T(8,128)(2,1)}, u32[]{:S(2)}, u32[]{:S(2)}) collective-permute-start(bf16[3,128,768]{2,1,0:T(8,128)(2,1)S(1)} %copy-done.8), channel_id=1, source_target_pairs={{0,16},{16,0},{1,17},{17,1},{2,18},{18,2},{3,19},{19,3},{4,20},{20... | collective-permute-start | bytes 1769480 | tf_op jit(solution)/shard_map/ppermute | solution.py:892
  274.0 24.9 %collective-permute-start.23 = (bf16[192,768]{1,0:T(8,128)(2,1)S(1)}, bf16[192,768]{1,0:T(8,128)(2,1)S(1)}, u32[]{:S(2)}, u32[]{:S(2)}) collective-permute-start(bf16[192,768]{1,0:T(8,128)(2,1)S(1)} %maximum_select_fusion.6), channel_id=1, source_target_pairs={{0,1},{1,0},{2,3},{3,2},{4,5},{5,4},{6,7},{7,6},{8,9},{9,8},{10,11... | collective-permute-start | bytes 884744 | tf_op jit(solution)/shard_map/ppermute | solution.py:902
  277.1 25.3 %collective-permute-start.32 = (bf16[4,96,768]{2,1,0:T(8,128)(2,1)S(1)}, bf16[4,96,768]{2,1,0:T(8,128)(2,1)S(1)}, u32[]{:S(2)}, u32[]{:S(2)}) collective-permute-start(bf16[4,96,768]{2,1,0:T(8,128)(2,1)S(1)} %get-tuple-element.99), channel_id=1, source_target_pairs={{0,2},{1,3},{2,0},{3,1},{4,6},{5,7},{6,4},{7,5},{8,10},{9,11},{10,... | collective-permute-start | bytes 1769480 | tf_op jit(solution)/shard_map/ppermute | solution.py:902
  285.8 20.4 %collective-permute-start.27 = (bf16[4,96,768]{2,1,0:T(8,128)(2,1)S(1)}, bf16[4,96,768]{2,1,0:T(8,128)(2,1)S(1)}, u32[]{:S(2)}, u32[]{:S(2)}) collective-permute-start(bf16[4,96,768]{2,1,0:T(8,128)(2,1)S(1)} %get-tuple-element.101), channel_id=1, source_target_pairs={{0,2},{1,3},{2,0},{3,1},{4,6},{5,7},{6,4},{7,5},{8,10},{9,11},{10,... | collective-permute-start | bytes 1769480 | tf_op jit(solution)/shard_map/ppermute | solution.py:902
  296.2 38.2 %collective-permute-start.10 = (bf16[384,2304]{1,0:T(8,128)(2,1)S(1)}, bf16[384,2304]{1,0:T(8,128)(2,1)}, u32[]{:S(2)}, u32[]{:S(2)}) collective-permute-start(bf16[384,2304]{1,0:T(8,128)(2,1)S(1)} %maximum_select_fusion.1), channel_id=1, source_target_pairs={{0,16},{16,0},{1,17},{17,1},{2,18},{18,2},{3,19},{19,3},{4,20},{20... | collective-permute-start | bytes 5308424 | tf_op jit(solution)/shard_map/ppermute | solution.py:892
  299.1 20.7 %collective-permute-start.24 = (bf16[384,768]{1,0:T(8,128)(2,1)S(1)}, bf16[384,768]{1,0:T(8,128)(2,1)}, u32[]{:S(2)}, u32[]{:S(2)}) collective-permute-start(bf16[384,768]{1,0:T(8,128)(2,1)S(1)} %maximum_select_fusion.4), channel_id=1, source_target_pairs={{0,16},{16,0},{1,17},{17,1},{2,18},{18,2},{3,19},{19,3},{4,20},{20... | collective-permute-start | bytes 1769480 | tf_op jit(solution)/shard_map/ppermute | solution.py:892
  303.2 13.0 %collective-permute-start.33 = (bf16[2,96,768]{2,1,0:T(8,128)(2,1)}, bf16[2,96,768]{2,1,0:T(8,128)(2,1)}, u32[]{:S(2)}, u32[]{:S(2)}) collective-permute-start(bf16[2,96,768]{2,1,0:T(8,128)(2,1)} %get-tuple-element.107), channel_id=1, source_target_pairs={{0,4},{1,5},{2,6},{3,7},{4,0},{5,1},{6,2},{7,3},{8,12},{9,13},{10,... | collective-permute-start | bytes 884744 | tf_op jit(solution)/shard_map/ppermute | solution.py:902
  307.1 15.5 %collective-permute-start.28 = (bf16[2,96,768]{2,1,0:T(8,128)(2,1)}, bf16[2,96,768]{2,1,0:T(8,128)(2,1)}, u32[]{:S(2)}, u32[]{:S(2)}) collective-permute-start(bf16[2,96,768]{2,1,0:T(8,128)(2,1)} %get-tuple-element.109), channel_id=1, source_target_pairs={{0,4},{1,5},{2,6},{3,7},{4,0},{5,1},{6,2},{7,3},{8,12},{9,13},{10,... | collective-permute-start | bytes 884744 | tf_op jit(solution)/shard_map/ppermute | solution.py:902
  317.2 9.3 %collective-permute-start.34 = (bf16[1,96,768]{2,1,0:T(8,128)(2,1)S(1)}, bf16[1,96,768]{2,1,0:T(8,128)(2,1)S(1)}, u32[]{:S(2)}, u32[]{:S(2)}) collective-permute-start(bf16[1,96,768]{2,1,0:T(8,128)(2,1)S(1)} %add_convert_fusion.22), channel_id=1, source_target_pairs={{0,8},{1,9},{2,10},{3,11},{4,12},{5,13},{6,14},{7,15},{8,0},{9,1},... | collective-permute-start | bytes 442376 | tf_op jit(solution)/shard_map/ppermute | solution.py:902
  323.6 9.2 %collective-permute-start.29 = (bf16[1,96,768]{2,1,0:T(8,128)(2,1)S(1)}, bf16[1,96,768]{2,1,0:T(8,128)(2,1)S(1)}, u32[]{:S(2)}, u32[]{:S(2)}) collective-permute-start(bf16[1,96,768]{2,1,0:T(8,128)(2,1)S(1)} %add_convert_fusion.24), channel_id=1, source_target_pairs={{0,8},{1,9},{2,10},{3,11},{4,12},{5,13},{6,14},{7,15},{8,0},{9,1},... | collective-permute-start | bytes 442376 | tf_op jit(solution)/shard_map/ppermute | solution.py:902
  (10 other events, 20.7 us)
